TPU v7x, 128 devices: a whole 4x4x4 slice. The times are simulated.
128 devices in a mesh: side: 2 (over core), row: 4 (over x), col: 16 (over y, z).
Axes of the slice: x: 4, y: 4, z: 4, core: 2. Of those that a mesh axis runs over, the one named last changes fastest.
Arguments:
- right_side: float32 [256, 512, 548], P('row', 'col', 'side'), may hold values from -24 to 24
- couplings: float32 [4, 256, 512], P(None, 'row', 'col'), may hold values from 0.04 to 0.2
- channel_rates: float32 [548], P('side'), may hold values from 0.2 to 1
- weight_in: float32 [548, 1024], replicated, may hold values from -0.25 to 0.25
- weight_mid: float32 [1024, 1024], replicated, may hold values from -0.1875 to 0.1875
- weight_out: float32 [1024, 616], replicated, may hold values from -0.1875 to 0.1875
- inverse_cov: float32 [616, 616], replicated, may hold values from -2 to 8, as said below
- profile_cells: int32 [2, 32768], P(None, ('row', 'col')), may hold values from 0 to 2047
- profile_counts: int32 [128], replicated, may hold values from 1 to 512, 16384 in all
- gate_first: bfloat16 [65536, 1024], P(('side', 'row', 'col')), may hold values from 0 to 1.09375
- gate_second: bfloat16 [65536, 1024], P(('side', 'row', 'col')), may hold values from 0 to 1.09375
Outputs:
- solution: float32 [256, 512, 548], P('row', 'col', 'side')
- residual: float32 [256, 512, 548], P('row', 'col', 'side')
Inputs may be any that keep to these rules, and one draw needn't show every extreme that they name: `profile_counts`: entry d counts the live profiles of device d in the order side, row, col; they fill its first slots. The entries add up to 16384, and the largest is 512. `profile_cells`: entry [s, t * 512 + i] is the cell, numbered latitude-major within tile t, observed by slot i of device s * 64 + t; entries of slots that are not live are unused. `inverse_cov`: symmetric positive definite.
All inputs are finite; a program needn't handle non-finite values.
Results may differ from a plain program's by a relative error of at most 0.0003.
Values may be sent and summed in bfloat16 or wider, within the bound.
No kernel may reach another device: no remote copies, remote signals or barrier semaphores. Data moves between devices by JAX's collectives and lax.ppermute only.
A program may use at most 128 MiB of HBM per device.

v0:
```python
import functools

import jax
import jax.numpy as jnp
from jax import lax
from jax.experimental import pallas as pl
from jax.experimental.pallas import tpu as pltpu
from jax.sharding import PartitionSpec as P

SCALE = 2.0**40
BLOCK = 256
f32, bf16 = jnp.float32, jnp.bfloat16
vmem = pl.BlockSpec(memory_space=pltpu.VMEM)
smem = pl.BlockSpec(memory_space=pltpu.SMEM)
hbm = pl.BlockSpec(memory_space=pl.ANY)


WIDE = 384
GROUP = 4


def shape(dims, dtype=f32):
    return jax.ShapeDtypeStruct(dims, dtype)


def call(kernel, out, in_specs, out_specs, scratch, mib, micros):
    return pl.pallas_call(
        kernel,
        out_shape=out,
        in_specs=in_specs,
        out_specs=out_specs,
        scratch_shapes=scratch,
        compiler_params=pltpu.CompilerParams(vmem_limit_bytes=mib << 20),
        cost_estimate=pl.CostEstimate(
            flops=int(micros * 1e9), bytes_accessed=int(micros * 3e6), transcendentals=0
        ),
    )


def halves_of(value):
    upper = value.astype(bf16)
    return upper, (value - upper.astype(f32)).astype(bf16)


def folded(value):
    rows, width = value.shape
    return jnp.sum(value.reshape(rows // 8, 8, width), axis=0)


def lane_vector(scalars):
    lane = lax.broadcasted_iota(jnp.int32, (8, 128), 1)
    result = jnp.zeros((8, 128), f32)
    for k, value in enumerate(scalars):
        result = jnp.where(lane == k, value, result)
    return result


def from_west(value, west_row, lon):
    last = value.shape[0] - 1
    return jnp.where(lon == 0, west_row, jnp.concatenate([value[last:], value[:last]], axis=0))


def from_east(value, east_row, lon):
    last = value.shape[0] - 1
    return jnp.where(lon == last, east_row, jnp.concatenate([value[1:], value[:1]], axis=0))


def sweep(lats, row, below, above, south, north, carry, after=None):
    def group(g, low, high, carry):
        for k in range(GROUP):
            i = g * GROUP + k
            under = south if low and k == 0 else below(i)
            over = north if high and k == GROUP - 1 else above(i)
            carry = row(i, under, over, carry)
        if after is not None:
            after(g)
        return carry

    last = lats // GROUP - 1
    carry = group(0, True, False, carry)
    carry = lax.fori_loop(1, last, lambda g, c: group(g, False, False, c), carry)
    return group(last, False, True, carry)


def prepare_kernel(
    side, w_in, w_mid, w_out, cov, in_hi, in_lo, mid_hi, mid_lo, out_hi, out_lo, cov_hi, cov_lo,
    s_in, s_cov, s_out, s_mid, sems
):
    sources = ((w_in, s_in), (cov, s_cov), (w_out, s_out), (w_mid, s_mid))
    copies = [pltpu.make_async_copy(a, b, sems.at[k]) for k, (a, b) in enumerate(sources)]
    for copy in copies:
        copy.start()
    for target in (in_hi, in_lo, out_hi, out_lo, cov_hi, cov_lo):
        target[...] = jnp.zeros_like(target)
    half = w_in.shape[0] // 2
    hidden = w_mid.shape[0]
    channels = cov.shape[0]

    def columns(total, step, move):
        def body(k, carry):
            move(pl.ds(pl.multiple_of(k * step, step), step))
            return carry

        lax.fori_loop(0, total // step, body, 0)
        if total % step:
            move(slice(total - total % step, total))

    copies[0].wait()
    for flag in range(2):

        @pl.when(side[0] == flag)
        def _(flag=flag):
            for target, source in ((0, flag * half), (WIDE, (1 - flag) * half)):

                def move(n, target=target, source=source):
                    upper, lower = halves_of(s_in[source : source + half, n])
                    in_hi[target : target + half, n] = upper
                    in_lo[target : target + half, n] = lower

                columns(hidden, 128, move)

    copies[1].wait()

    def move_cov(n):
        upper, lower = halves_of(s_cov[:, n])
        cov_hi[:channels, n] = upper
        cov_lo[:channels, n] = lower

    columns(channels, 128, move_cov)
    copies[2].wait()

    def move_out(n):
        upper, lower = halves_of(s_out[:, n])
        out_hi[:channels, n] = upper
        out_lo[:channels, n] = lower

    columns(hidden, 128, move_out)
    copies[3].wait()

    def move_mid(n):
        upper, lower = halves_of(s_mid[n, :])
        mid_hi[n, :] = upper
        mid_lo[n, :] = lower

    columns(hidden, 64, move_mid)


def prepare_call(side, w_in, w_mid, w_out, cov, channels):
    hidden = w_mid.shape[0]
    dims = [(2 * WIDE, hidden), (hidden, hidden), (channels, hidden), (channels, channels)]
    out = [shape(d, bf16) for d in dims for _ in range(2)]
    return call(
        prepare_kernel,
        out,
        [smem] + [hbm] * 4,
        [vmem] * 8,
        [pltpu.VMEM(m.shape, f32) for m in (w_in, cov, w_out, w_mid)]
        + [pltpu.SemaphoreType.DMA((4,))],
        16,
        5,
    )(side, w_in, w_mid, w_out, cov)


def tangent_kernel(
    with_square, cells, counts, field, south, north, west, east, coupling, rates, own, other, *rest
):
    image = rest[-1]
    lats, lons, width = field.shape
    rate = rates[...]
    tail = width - 256
    lon = lax.broadcasted_iota(jnp.int32, (lons, width), 0)
    image[2] = jnp.zeros_like(image[2])

    def row(i, below, above, total):
        value = field[i]
        c = coupling[i]
        to_west = from_west(value, west[pl.ds(i, 1), :], lon)
        to_east = from_east(value, east[pl.ds(i, 1), :], lon)
        flux = c[:, 0:1] * (to_east - value)
        flux = flux + c[:, 1:2] * (to_west - value)
        flux = flux + c[:, 2:3] * (above - value)
        flux = flux + c[:, 3:4] * (below - value)
        result = value + rate * flux
        rows = pl.ds(i * lons if isinstance(i, int) else pl.multiple_of(i * lons, lons), lons)
        image[0, rows, :] = result[:, 0:128]
        image[1, rows, :] = result[:, 128:256]
        image[2, rows, 0:tail] = result[:, 256:]
        if with_square:
            total = total + folded(value * value)
        return total

    total = jnp.zeros((8, width), f32)
    total = sweep(
        lats, row, lambda i: field[i - 1], lambda i: field[i + 1], south[0], north[0], total
    )
    if with_square:
        rest[0][...] = lane_vector([jnp.sum(total)])

    def gather(which, out):
        def body(b, carry):
            first = pl.multiple_of(b * 8, 8)
            found = [cells[which, first + k] for k in range(8)]
            rows = [[image[t, pl.ds(cell, 1), :] for t in range(3)] for cell in found]
            for k in range(8):
                out[pl.ds(first + k, 1), :] = jnp.concatenate(rows[k], axis=1)
            return carry

        lax.fori_loop(0, (counts[which] + 7) // 8, body, 0)

    gather(1, other)
    gather(0, own)


def tangent_call(with_square, cells, counts, field, halo, coupling, rates):
    lats, lons, width = field.shape
    slots = cells.shape[1]
    out = [shape((slots, WIDE))] * 2 + [shape((8, 128))] * with_square
    return call(
        functools.partial(tangent_kernel, with_square),
        out,
        [smem, smem] + [vmem] * 7,
        [vmem] * len(out),
        [pltpu.VMEM((3, lats * lons, 128), f32)],
        8,
        6,
    )(cells, counts, field, *halo, coupling, rates)


def tile(left, right, n, transposed):
    hi, lo = left
    if transposed:
        pick = [w[pl.ds(n, BLOCK), :] for w in right]
        dims = (((1,), (1,)), ((), ()))
    else:
        pick = [w[:, pl.ds(n, BLOCK)] for w in right]
        dims = (((1,), (0,)), ((), ()))
    dot = functools.partial(lax.dot_general, dimension_numbers=dims, preferred_element_type=f32)
    upper = hi[...]
    return dot(upper, pick[0]) + dot(upper, pick[1]) + dot(lo[...], pick[0])


def layer(left, right, columns, transposed, finish, carry=0):
    def body(k, carry):
        n = pl.multiple_of(k * BLOCK, BLOCK)
        return finish(n, tile(left, right, n, transposed), carry)

    return lax.fori_loop(0, columns // BLOCK, body, carry)


def gated(gate, target):
    def finish(n, value, carry):
        upper, lower = halves_of(value * gate[:, pl.ds(n, BLOCK)].astype(f32))
        target[0][:, pl.ds(n, BLOCK)] = upper
        target[1][:, pl.ds(n, BLOCK)] = lower
        return carry

    return finish


def forward_kernel(
    with_sums, counts, own, other, gate_one, gate_two,
    in_hi, in_lo, mid_hi, mid_lo, out_hi, out_lo, cov_hi, cov_lo, *rest
):
    if with_sums:
        sums_in, z_hi, z_lo, sums = rest[:4]
    else:
        z_hi, z_lo = rest[:2]
    x_hi, x_lo, a_hi, a_lo, b_hi, b_lo, t_full, t_hi, t_lo = rest[-9:]
    rows = own.shape[0]
    for start, part in ((0, own), (WIDE, other)):
        upper, lower = halves_of(part[...])
        x_hi[:, start : start + WIDE] = upper
        x_lo[:, start : start + WIDE] = lower
    hidden = mid_hi.shape[0]
    channels = cov_hi.shape[0]
    layer((x_hi, x_lo), (in_hi, in_lo), hidden, False, gated(gate_one, (a_hi, a_lo)))
    layer((a_hi, a_lo), (mid_hi, mid_lo), hidden, False, gated(gate_two, (b_hi, b_lo)))

    def keep_outputs(n, value, carry):
        if with_sums:
            t_full[:, pl.ds(n, BLOCK)] = value
        upper, lower = halves_of(value)
        t_hi[:, pl.ds(n, BLOCK)] = upper
        t_lo[:, pl.ds(n, BLOCK)] = lower
        return carry

    layer((b_hi, b_lo), (out_hi, out_lo), channels, True, keep_outputs)
    live = lax.broadcasted_iota(jnp.int32, (rows, BLOCK), 0) < counts[0]

    def keep_weighted(n, value, carry):
        upper, lower = halves_of(value)
        z_hi[:, pl.ds(n, BLOCK)] = upper
        z_lo[:, pl.ds(n, BLOCK)] = lower
        if with_sums:
            carry = carry + folded(jnp.where(live, value * t_full[:, pl.ds(n, BLOCK)], 0.0))
        return carry

    total = jnp.zeros((8, BLOCK), f32)
    total = layer((t_hi, t_lo), (cov_hi, cov_lo), channels, False, keep_weighted, total)
    if with_sums:
        lane = lax.broadcasted_iota(jnp.int32, (8, 128), 1)
        sums[...] = jnp.where(lane == 3, jnp.sum(total), sums_in[...])


def backward_kernel(
    scale, z_hi, z_lo, gate_one, gate_two, in_hi, in_lo, mid_hi, mid_lo, out_hi, out_lo,
    own_grad, other_grad, a_hi, a_lo, b_hi, b_lo
):
    hidden = mid_hi.shape[0]
    layer((z_hi, z_lo), (out_hi, out_lo), hidden, False, gated(gate_two, (a_hi, a_lo)))
    layer((a_hi, a_lo), (mid_hi, mid_lo), hidden, True, gated(gate_one, (b_hi, b_lo)))
    for start in range(0, 2 * WIDE, BLOCK):
        value = tile((b_hi, b_lo), (in_hi, in_lo), start, True)
        for first, target in ((0, own_grad), (WIDE, other_grad)):
            low, top = max(start, first), min(start + BLOCK, first + WIDE)
            if low < top:
                target[:, low - first : top - first] = value[:, low - start : top - start] * scale


def forward_call(counts, own, other, gates, weights, sums):
    rows = own.shape[0]
    hidden, channels = weights[2].shape[0], weights[6].shape[0]
    with_sums = sums is not None
    out = [shape((rows, channels), bf16)] * 2 + [shape((8, 128))] * with_sums
    pair = lambda n: [pltpu.VMEM((rows, n), bf16)] * 2
    args = (counts, own, other, *gates, *weights) + ((sums,) if with_sums else ())
    return call(
        functools.partial(forward_kernel, with_sums),
        out,
        [smem] + [vmem] * (len(args) - 1),
        [vmem] * len(out),
        pair(2 * WIDE)
        + pair(hidden)
        + pair(hidden)
        + [pltpu.VMEM((rows, channels), f32)]
        + pair(channels),
        16,
        13,
    )(*args)


def backward_call(scale, z, gates, weights):
    rows = z[0].shape[0]
    hidden = weights[2].shape[0]
    args = (*z, *gates, *weights[:6])
    return call(
        functools.partial(backward_kernel, scale),
        [shape((rows, WIDE))] * 2,
        [vmem] * len(args),
        [vmem] * 2,
        [pltpu.VMEM((rows, hidden), bf16)] * 4,
        10,
        11,
    )(*args)


def spread_kernel(counts, cells, own, other, coupling, edge, field, south, north, west, east, parts):
    lats, lons, width = field.shape
    slots = own.shape[0]
    chunk = 512
    for k, part in enumerate((own, other)):
        row = lax.broadcasted_iota(jnp.int32, (slots, WIDE), 0)
        upper, lower = halves_of(jnp.where(row < counts[k], part[...], 0.0))
        parts[k, :, 0:WIDE] = upper
        parts[k, :, WIDE : 2 * WIDE] = lower

    def body(b, carry):
        first = b * chunk
        cell = lax.broadcasted_iota(jnp.int32, (chunk, BLOCK), 0) + first
        lat = pl.ds(b * (chunk // lons), chunk // lons)

        def piece(k, s):
            hot = (cell == cells[k : k + 1, s : s + BLOCK]).astype(f32).astype(bf16)
            both = jnp.dot(hot, parts[k, s : s + BLOCK, :], preferred_element_type=f32)
            total = both[:, :WIDE] + both[:, WIDE:]
            return total[:, :width].reshape(chunk // lons, lons, width)

        field[lat] = piece(0, 0) + piece(1, 0)
        for k in range(2):
            for s in range(BLOCK, slots, BLOCK):

                @pl.when(counts[k] > s)
                def _(k=k, s=s):
                    field[lat] += piece(k, s)

        return carry

    lax.fori_loop(0, lats * lons // chunk, body, 0)

    def move(b, carry):
        for k in range(8):
            i = b * 8 + k
            value = field[i]
            west[pl.ds(i, 1), :] = value[:1]
            east[pl.ds(i, 1), :] = value[lons - 1 :]
        return carry

    lax.fori_loop(0, lats // 8, move, 0)
    east[...] = east[...] * edge[:, 0:1]
    west[...] = west[...] * edge[:, 1:2]
    south[0] = field[0] * coupling[0][:, 3:4]
    north[0] = field[lats - 1] * coupling[lats - 1][:, 2:3]


def edge_shapes(lats, lons, width):
    return [shape((1, lons, width))] * 2 + [shape((lats, width))] * 2


def spread_call(counts, cells, own, other, coupling, edge, width):
    lats, lons, _ = coupling.shape
    slots = own.shape[0]
    out = [shape((lats, lons, width))] + edge_shapes(lats, lons, width)
    return call(
        spread_kernel,
        out,
        [smem] + [vmem] * 5,
        [vmem] * 5,
        [pltpu.VMEM((2, slots, 2 * WIDE), bf16)],
        10,
        5,
    )(counts, cells, own, other, coupling, edge)


def adjoint_rows(field, south, north, west, east, coupling, rates, finish, carry, after=None):
    lats, lons, width = field.shape
    rate = rates[...]
    lon = lax.broadcasted_iota(jnp.int32, (lons, width), 0)

    def row(i, below, above, carry):
        value = field[i]
        c = coupling[i]
        flux = below + above
        flux = flux + from_west(c[:, 0:1] * value, west[pl.ds(i, 1), :], lon)
        flux = flux + from_east(c[:, 1:2] * value, east[pl.ds(i, 1), :], lon)
        total = c[:, 0:1] + c[:, 1:2] + c[:, 2:3] + c[:, 3:4]
        return finish(i, value + rate * (flux - total * value), carry)

    def below(i):
        return coupling[i - 1][:, 2:3] * field[i - 1]

    def above(i):
        return coupling[i + 1][:, 3:4] * field[i + 1]

    return sweep(lats, row, below, above, south[0], north[0], carry, after)


def basis_kernel(
    field, south, north, west, east, coupling, rates, right_side, sums_in,
    basis, out_south, out_north, out_west, out_east, sums
):
    lats, lons, width = field.shape

    def finish(i, value, carry):
        basis[i] = value
        out_west[pl.ds(i, 1), :] = value[:1]
        out_east[pl.ds(i, 1), :] = value[lons - 1 :]
        return carry[0] + folded(right_side[i] * value), carry[1] + folded(value * value)

    zero = jnp.zeros((8, width), f32)
    cross, square = adjoint_rows(
        field, south, north, west, east, coupling, rates, finish, (zero, zero)
    )
    out_south[0] = basis[0]
    out_north[0] = basis[lats - 1]
    lane = lax.broadcasted_iota(jnp.int32, (8, 128), 1)
    result = jnp.where(lane == 1, jnp.sum(cross), sums_in[...])
    sums[...] = jnp.where(lane == 2, jnp.sum(square), result)


def basis_call(field, halo, coupling, rates, right_side, sums):
    lats, lons, width = field.shape
    out = [shape((lats, lons, width))] + edge_shapes(lats, lons, width) + [shape((8, 128))]
    return call(basis_kernel, out, [vmem] * 9, [vmem] * 6, [], 6, 4)(
        field, *halo, coupling, rates, right_side, sums
    )


def final_kernel(
    field, south, north, west, east, coupling, rates, right_side, basis, sums,
    solution_out, residual_out, solution_part, residual_part, sems
):
    lats, lons, width = field.shape
    s = sums[0:1, :]
    rr, rv, vv, vy = s[:, 0:1], s[:, 1:2], s[:, 2:3], s[:, 3:4]
    q = SCALE * rv
    den = rr + q
    first_step = rr / den
    p = SCALE * first_step
    rest = q / den
    new = p * p * vv - rest * rest * rr
    a = rest + new / rr
    square = a * a * rr - 2.0 * a * p * rv + p * p * vv
    curve = a * a * q - 2.0 * a * p * (SCALE * vv) + p * p * vy
    step = new / (square + curve)
    k_right = first_step + step * a
    k_basis = -(step * p)
    l_right = rest - step * a
    l_basis = step * p - p - step * a * SCALE
    l_image = step * p
    outs = ((solution_part, solution_out), (residual_part, residual_out))

    def finish(i, value, carry):
        solution_part[i] = k_right * right_side[i] + k_basis * basis[i]
        residual_part[i] = l_right * right_side[i] + l_basis * basis[i] + l_image * value
        return carry

    def start(g):
        rows = pl.ds(g * GROUP, GROUP)
        for k, (part, out) in enumerate(outs):
            pltpu.make_async_copy(part.at[rows], out.at[rows], sems.at[k]).start()

    def after(g):
        if not isinstance(g, int) or g > 0:
            start(g - 1)

    adjoint_rows(field, south, north, west, east, coupling, rates, finish, 0, after)
    start(lats // GROUP - 1)
    for k, (part, out) in enumerate(outs):
        pltpu.make_async_copy(part, out, sems.at[k]).wait()


def final_call(field, halo, coupling, rates, right_side, basis, sums):
    return call(
        final_kernel,
        [shape(field.shape)] * 2,
        [vmem] * 10,
        [hbm] * 2,
        [pltpu.VMEM(field.shape, f32)] * 2 + [pltpu.SemaphoreType.DMA((2,))],
        12,
        6,
    )(field, *halo, coupling, rates, right_side, basis, sums)


def shifted(value, axis, step):
    count = lax.axis_size(axis)
    return lax.ppermute(value, axis, [(i, (i + step) % count) for i in range(count)])


def exchanged(south_row, north_row, west_col, east_col):
    from_west = shifted(east_col, "col", 1)
    from_east = shifted(west_col, "col", -1)
    from_south = shifted(north_row, "row", 1)
    from_north = shifted(south_row, "row", -1)
    return from_south, from_north, from_west, from_east


def swapped(value):
    return lax.ppermute(value, "side", [(0, 1), (1, 0)])


def everyone(values):
    n = 4
    total = values + swapped(values)
    total = total + sum(shifted(total, "row", k) for k in range(1, n))
    size = lax.axis_size("col")
    for low in (True, False):
        base = total
        for k in range(1, n):
            if low:
                pairs = [(c, (c // n) * n + (c % n + k) % n) for c in range(size)]
            else:
                pairs = [(c, ((c // n + k) % n) * n + c % n) for c in range(size)]
            total = total + lax.ppermute(base, "col", pairs)
    return total


def local(
    right_side,
    couplings,
    channel_rates,
    weight_in,
    weight_mid,
    weight_out,
    inverse_cov,
    profile_cells,
    profile_counts,
    gate_first,
    gate_second,
):
    side_index = lax.axis_index("side")
    tile_count = lax.axis_size("row") * lax.axis_size("col")
    tile_index = lax.axis_index("row") * lax.axis_size("col") + lax.axis_index("col")
    lats, lons, width = right_side.shape
    halo = exchanged(
        right_side[:1], right_side[lats - 1 :], right_side[:, 0], right_side[:, lons - 1]
    )
    latitude = lax.axis_index("row") * lats + jnp.arange(lats)
    north_open = (latitude < lats * lax.axis_size("row") - 1)[:, None]
    south_open = (latitude > 0)[:, None]
    planes = [
        couplings[0],
        couplings[1],
        jnp.where(north_open, couplings[2], 0.0),
        jnp.where(south_open, couplings[3], 0.0),
    ]
    coupling = jnp.stack(planes, axis=2)
    edge = jnp.stack([couplings[0, :, lons - 1], couplings[1, :, 0]], axis=1)
    rates = channel_rates[None, :]
    order = jnp.stack([side_index, 1 - side_index])
    cells = jnp.clip(profile_cells[order], 0, lats * lons - 1)
    counts = profile_counts[order * tile_count + tile_index]
    weights = prepare_call(
        order[:1], weight_in, weight_mid, weight_out.T, inverse_cov, 3 * BLOCK
    )
    gates = (gate_first, gate_second)

    own, other, sums = tangent_call(True, cells, counts, right_side, halo, coupling, rates)
    z = forward_call(counts, own, swapped(other), gates, weights, None)
    own, other = backward_call(1.0 / SCALE, z, gates, weights)
    field, *out = spread_call(counts, cells, own, swapped(other), coupling, edge, width)
    halo = exchanged(*out)
    basis, *out, sums = basis_call(field, halo, coupling, rates, right_side, sums)
    halo = exchanged(*out)
    own, other = tangent_call(False, cells, counts, basis, halo, coupling, rates)
    *z, sums = forward_call(counts, own, swapped(other), gates, weights, sums)
    sums = everyone(sums)
    own, other = backward_call(1.0, z, gates, weights)
    field, *out = spread_call(counts, cells, own, swapped(other), coupling, edge, width)
    halo = exchanged(*out)
    return tuple(final_call(field, halo, coupling, rates, right_side, basis, sums))


def solution(mesh):
    in_specs = (
        P("row", "col", "side"),
        P(None, "row", "col"),
        P("side"),
        P(),
        P(),
        P(),
        P(),
        P(None, ("row", "col")),
        P(),
        P(("side", "row", "col"), None),
        P(("side", "row", "col"), None),
    )
    out_specs = (P("row", "col", "side"), P("row", "col", "side"))
    return jax.shard_map(local, mesh=mesh, in_specs=in_specs, out_specs=out_specs, check_vma=False)
```

profile of v0, /device:TPU:0, one launch (start us, length us, event | category | flops | bytes accessed | tf_op | source)
XLA Modules:
  0.0 163.6 jit_solution(4319549073860990081)
XLA Ops:
  1.5 2.9 %collective-permute-start.1 = (f32[1,32,274]{2,1,0:T(8,128)S(1)}, f32[1,32,274]{2,1,0:T(8,128)S(1)}, u32[]{:S(2)}, u32[]{:S(2)}) collective-permute-start(f32[1,32,274]{2,1,0:T(8,128)S(1)} %get-tuple-element.80), channel_id=1, source_target_pairs={{0,48},{16,0},{32,16},{48,32},{1,49},{17,1},{33,17},{49,33},{2,50}... | collective-permute-start | bytes 105224 | tf_op jit(solution)/shard_map/ppermute | solution.py:536
  8.0 4.7 %collective-permute-start.3 = (f32[64,274]{1,0:T(8,128)S(1)}, f32[64,274]{1,0:T(8,128)S(1)}, u32[]{:S(2)}, u32[]{:S(2)}) collective-permute-start(f32[64,274]{1,0:T(8,128)S(1)} %bitcast.28), channel_id=1, source_target_pairs={{0,15},{1,0},{2,1},{3,2},{4,3},{5,4},{6,5},{7,6},{8,7},{9,8},{10,9... | collective-permute-start | bytes 210440 | tf_op jit(solution)/shard_map/ppermute | solution.py:536
  19.0 6.1 %shard_map.122 = (f32[512,384]{1,0:T(8,128)S(1)}, f32[512,384]{1,0:T(8,128)S(1)}, f32[8,128]{1,0:T(8,128)S(1)}) custom-call(s32[2,512]{1,0:T(2,128)S(1)} %broadcast_clamp_fusion.cells, s32[2]{0:T(128)S(1)} %gather_fusion, f32[64,32,274]{2,1,0:T(8,128)S(1)} %copy-done.1, f32[1,32,274]{2,1,0:T(8,128)S(1)} %collective-permute-done.south, ...), custom_call_target="tpu_custom_call" | custom-call | flops 6000000000 | bytes 18000000 | tf_op jit(solution)/shard_map/pallas_call | solution.py:218
  25.3 4.4 %shard_map.123 = (bf16[768,1024]{1,0:T(8,128)(2,1)S(1)}, bf16[768,1024]{1,0:T(8,128)(2,1)S(1)}, bf16[1024,1024]{1,0:T(8,128)(2,1)S(1)}, bf16[1024,1024]{1,0:T(8,...) custom-call(s32[1]{0:T(128)} %bitcast.10.side, ...), custom_call_target="tpu_custom_call" | custom-call | flops 5000000000 | bytes 15000000 | tf_op jit(solution)/shard_map/pallas_call | solution.py:152
  29.8 13.4 %shard_map.124 = (bf16[512,768]{1,0:T(8,128)(2,1)S(1)}, bf16[512,768]{1,0:T(8,128)(2,1)S(1)}) custom-call(s32[2]{0:T(128)S(1)} %gather_fusion, f32[512,384]{1,0:T(8,128)S(1)} %get-tuple-element.40.own, f32[512,384]{1,0:T(8,128)S(1)} %collective-permute-done.4.other, bf16[512,1024]{1,0:T(8,128)(2,1)S(1)} %copy-done.7, bf16[512,1024]{1,0:T(8,128)(2,1)S(1)} %copy-done.9, ...), custom_call_target="tpu_custom_call" | custom-call | flops 12999999488 | bytes 39000000 | tf_op jit(solution)/shard_map/pallas_call | solution.py:327
  43.3 9.9 %shard_map.125 = (f32[512,384]{1,0:T(8,128)S(1)}, f32[512,384]{1,0:T(8,128)S(1)}) custom-call(bf16[512,768]{1,0:T(8,128)(2,1)S(1)} %get-tuple-element.50.z_hi, bf16[512,768]{1,0:T(8,128)(2,1)S(1)} %get-tuple-element.51.z_lo, bf16[512,1024]{1,0:T(8,128)(2,1)S(1)} %copy-done.7, bf16[512,1024]{1,0:T(8,128)(2,1)S(1)} %copy-done.9, ...), custom_call_target="tpu_custom_call" | custom-call | flops 11000000512 | bytes 33000000 | tf_op jit(solution)/shard_map/pallas_call | solution.py:346
  55.8 4.9 %shard_map.126 = (f32[64,32,274]{2,1,0:T(8,128)S(1)}, f32[1,32,274]{2,1,0:T(8,128)S(1)}, f32[1,32,274]{2,1,0:T(8,128)S(1)}, f32[64,274]{1,0:T(8,128)S(1)}, f32[64,274]{1,0:T(8,128)S(1)}) custom-call(s32[2]{0:T(128)S(1)} %gather_fusion, s32[2,512]{1,0:T(2,128)S(1)} %broadcast_clamp_fusion.cells, f32[512,384]{1,0:T(8,128)S(1)} %get-tuple-element.52.own, ...), custom_call_target="tpu_custom_call" | custom-call | flops 5000000000 | bytes 15000000 | tf_op jit(solution)/shard_map/pallas_call | solution.py:413
  60.9 5.3 %collective-permute-start.9 = (f32[64,274]{1,0:T(8,128)S(1)}, f32[64,274]{1,0:T(8,128)S(1)}, u32[]{:S(2)}, u32[]{:S(2)}) collective-permute-start(f32[64,274]{1,0:T(8,128)S(1)} %get-tuple-element.58), channel_id=1, source_target_pairs={{0,15},{1,0},{2,1},{3,2},{4,3},{5,4},{6,5},{7,6},{8,7},{9,8},{10,9... | collective-permute-start | bytes 210440 | tf_op jit(solution)/shard_map/ppermute | solution.py:536
  66.2 3.2 %collective-permute-start.7 = (f32[1,32,274]{2,1,0:T(8,128)S(1)}, f32[1,32,274]{2,1,0:T(8,128)S(1)}, u32[]{:S(2)}, u32[]{:S(2)}) collective-permute-start(f32[1,32,274]{2,1,0:T(8,128)S(1)} %get-tuple-element.56), channel_id=1, source_target_pairs={{0,48},{16,0},{32,16},{48,32},{1,49},{17,1},{33,17},{49,33},{2,50}... | collective-permute-start | bytes 105224 | tf_op jit(solution)/shard_map/ppermute | solution.py:536
  69.4 2.1 %collective-permute-done.6.south = f32[1,32,274]{2,1,0:T(8,128)S(1)} collective-permute-done((f32[1,32,274]{2,1,0:T(8,128)S(1)}, f32[1,32,274]{2,1,0:T(8,128)S(1)}, u32[]{:S(2)}, u32[]{:S(2)}) %collective-permute-start.6) | collective-permute-done | bytes 35104 | tf_op jit(solution)/shard_map/ppermute | solution.py:536
  71.5 6.1 %shard_map.127 = (f32[64,32,274]{2,1,0:T(8,128)S(1)}, f32[1,32,274]{2,1,0:T(8,128)S(1)}, f32[1,32,274]{2,1,0:T(8,128)S(1)}, f32[64,274]{1,0:T(8,128)S(1)}, f32[64,274]{1,0:T(8,128)S(1)}, /*index=5*/f32[8,128]{1,0:T(8,128)S(1)}) custom-call(f32[64,32,274]{2,1,0:T(8,128)S(1)} %get-tuple-element.54.field, f32[1,32,274]{2,1,0:T(8,128)S(1)} %collective-permute-done.6.south, ...), custom_call_target="tpu_custom_call" | custom-call | flops 4000000000 | bytes 12000000 | tf_op jit(solution)/shard_map/pallas_call | solution.py:473
  77.7 5.3 %collective-permute-start.13 = (f32[64,274]{1,0:T(8,128)S(1)}, f32[64,274]{1,0:T(8,128)S(1)}, u32[]{:S(2)}, u32[]{:S(2)}) collective-permute-start(f32[64,274]{1,0:T(8,128)S(1)} %get-tuple-element.64), channel_id=1, source_target_pairs={{0,15},{1,0},{2,1},{3,2},{4,3},{5,4},{6,5},{7,6},{8,7},{9,8},{10,9... | collective-permute-start | bytes 210440 | tf_op jit(solution)/shard_map/ppermute | solution.py:536
  86.3 2.1 %collective-permute-done.10.south = f32[1,32,274]{2,1,0:T(8,128)S(1)} collective-permute-done((f32[1,32,274]{2,1,0:T(8,128)S(1)}, f32[1,32,274]{2,1,0:T(8,128)S(1)}, u32[]{:S(2)}, u32[]{:S(2)}) %collective-permute-start.10) | collective-permute-done | bytes 35104 | tf_op jit(solution)/shard_map/ppermute | solution.py:536
  88.5 6.0 %shard_map.128 = (f32[512,384]{1,0:T(8,128)S(1)}, f32[512,384]{1,0:T(8,128)S(1)}) custom-call(s32[2,512]{1,0:T(2,128)S(1)} %broadcast_clamp_fusion.cells, s32[2]{0:T(128)S(1)} %gather_fusion, f32[64,32,274]{2,1,0:T(8,128)S(1)} %get-tuple-element.60.field.basis, f32[1,32,274]{2,1,0:T(8,128)S(1)} %collective-permute-done.10.south, ...), custom_call_target="tpu_custom_call" | custom-call | flops 6000000000 | bytes 18000000 | tf_op jit(solution)/shard_map/pallas_call | solution.py:218
  94.6 2.3 %collective-permute-done.14.other = f32[512,384]{1,0:T(8,128)S(1)} collective-permute-done((f32[512,384]{1,0:T(8,128)S(1)}, f32[512,384]{1,0:T(8,128)S(1)}, u32[]{:S(2)}, u32[]{:S(2)}) %collective-permute-start.14) | collective-permute-done | bytes 786464 | tf_op jit(solution)/shard_map/ppermute | solution.py:548
  97.0 13.6 %shard_map.129 = (bf16[512,768]{1,0:T(8,128)(2,1)S(1)}, bf16[512,768]{1,0:T(8,128)(2,1)S(1)}, f32[8,128]{1,0:T(8,128)S(1)}) custom-call(s32[2]{0:T(128)S(1)} %gather_fusion, f32[512,384]{1,0:T(8,128)S(1)} %get-tuple-element.65.own, f32[512,384]{1,0:T(8,128)S(1)} %collective-permute-done.14.other, bf16[512,1024]{1,0:T(8,128)(2,1)S(1)} %copy-done.8, ...), custom_call_target="tpu_custom_call" | custom-call | flops 12999999488 | bytes 39000000 | tf_op jit(solution)/shard_map/pallas_call | solution.py:327
  110.6 9.9 %shard_map.130 = (f32[512,384]{1,0:T(8,128)S(1)}, f32[512,384]{1,0:T(8,128)S(1)}) custom-call(bf16[512,768]{1,0:T(8,128)(2,1)S(1)} %get-tuple-element.68.z_hi, bf16[512,768]{1,0:T(8,128)(2,1)S(1)} %get-tuple-element.69.z_lo, bf16[512,1024]{1,0:T(8,128)(2,1)S(1)} %copy-done.8, bf16[512,1024]{1,0:T(8,128)(2,1)S(1)} %copy-done.10, ...), custom_call_target="tpu_custom_call" | custom-call | flops 11000000512 | bytes 33000000 | tf_op jit(solution)/shard_map/pallas_call | solution.py:346
  122.9 3.0 %collective-permute-start.23 = (f32[8,128]{1,0:T(8,128)S(1)}, f32[8,128]{1,0:T(8,128)S(1)}, u32[]{:S(2)}, u32[]{:S(2)}) collective-permute-start(f32[8,128]{1,0:T(8,128)S(1)} %add.86), channel_id=1, source_target_pairs={{0,48},{16,0},{32,16},{48,32},{1,49},{17,1},{33,17},{49,33},{2,50}... | collective-permute-start | bytes 12296 | tf_op jit(solution)/shard_map/ppermute | solution.py:536
  127.2 3.8 %collective-permute-done.22 = f32[8,128]{1,0:T(8,128)S(1)} collective-permute-done((f32[8,128]{1,0:T(8,128)S(1)}, f32[8,128]{1,0:T(8,128)S(1)}, u32[]{:S(2)}, u32[]{:S(2)}) %collective-permute-start.22) | collective-permute-done | bytes 4128 | tf_op jit(solution)/shard_map/ppermute | solution.py:536
  140.4 4.9 %shard_map.131 = (f32[64,32,274]{2,1,0:T(8,128)S(1)}, f32[1,32,274]{2,1,0:T(8,128)S(1)}, f32[1,32,274]{2,1,0:T(8,128)S(1)}, f32[64,274]{1,0:T(8,128)S(1)}, f32[64,274]{1,0:T(8,128)S(1)}) custom-call(s32[2]{0:T(128)S(1)} %gather_fusion, s32[2,512]{1,0:T(2,128)S(1)} %broadcast_clamp_fusion.cells, f32[512,384]{1,0:T(8,128)S(1)} %get-tuple-element.70.own, ...), custom_call_target="tpu_custom_call" | custom-call | flops 5000000000 | bytes 15000000 | tf_op jit(solution)/shard_map/pallas_call | solution.py:413
  145.4 3.2 %collective-permute-start.17 = (f32[1,32,274]{2,1,0:T(8,128)S(1)}, f32[1,32,274]{2,1,0:T(8,128)S(1)}, u32[]{:S(2)}, u32[]{:S(2)}) collective-permute-start(f32[1,32,274]{2,1,0:T(8,128)S(1)} %get-tuple-element.74), channel_id=1, source_target_pairs={{0,48},{16,0},{32,16},{48,32},{1,49},{17,1},{33,17},{49,33},{2,50}... | collective-permute-start | bytes 105224 | tf_op jit(solution)/shard_map/ppermute | solution.py:536
  148.6 5.3 %collective-permute-start.19 = (f32[64,274]{1,0:T(8,128)S(1)}, f32[64,274]{1,0:T(8,128)S(1)}, u32[]{:S(2)}, u32[]{:S(2)}) collective-permute-start(f32[64,274]{1,0:T(8,128)S(1)} %get-tuple-element.76), channel_id=1, source_target_pairs={{0,15},{1,0},{2,1},{3,2},{4,3},{5,4},{6,5},{7,6},{8,7},{9,8},{10,9... | collective-permute-start | bytes 210440 | tf_op jit(solution)/shard_map/ppermute | solution.py:536
  154.0 2.6 %collective-permute-done.18.west = f32[64,274]{1,0:T(8,128)S(1)} collective-permute-done((f32[64,274]{1,0:T(8,128)S(1)}, f32[64,274]{1,0:T(8,128)S(1)}, u32[]{:S(2)}, u32[]{:S(2)}) %collective-permute-start.18) | collective-permute-done | bytes 70176 | tf_op jit(solution)/shard_map/ppermute | solution.py:536
  156.6 6.9 %shard_map.132 = (f32[64,32,274]{2,1,0:T(8,128)}, f32[64,32,274]{2,1,0:T(8,128)}) custom-call(f32[64,32,274]{2,1,0:T(8,128)S(1)} %get-tuple-element.72.field, f32[1,32,274]{2,1,0:T(8,128)S(1)} %collective-permute-done.16.south, f32[1,32,274]{2,1,0:T(8,128)S(1)} %collective-permute-done.17.north, f32[64,274]{1,0:T(8,128)S(1)} %collective-permute-done.18.west, ...), custom_call_target="tpu_custom_call" | custom-call | flops 6000000000 | bytes 18000000 | tf_op jit(solution)/shard_map/pallas_call | solution.py:523
  (126 shorter events, 30.2 us)
Async XLA Ops:
  1.5 15.6 %collective-permute-start.1 = (f32[1,32,274]{2,1,0:T(8,128)S(1)}, f32[1,32,274]{2,1,0:T(8,128)S(1)}, u32[]{:S(2)}, u32[]{:S(2)}) collective-permute-start(f32[1,32,274]{2,1,0:T(8,128)S(1)} %get-tuple-element.80), channel_id=1, source_target_pairs={{0,48},{16,0},{32,16},{48,32},{1,49},{17,1},{33,17},{49,33},{2,50}... | collective-permute-start | bytes 105224 | tf_op jit(solution)/shard_map/ppermute | solution.py:536
  4.4 12.7 %collective-permute-start = (f32[1,32,274]{2,1,0:T(8,128)S(1)}, f32[1,32,274]{2,1,0:T(8,128)S(1)}, u32[]{:S(2)}, u32[]{:S(2)}) collective-permute-start(f32[1,32,274]{2,1,0:T(8,128)S(1)} %get-tuple-element.81), channel_id=1, source_target_pairs={{0,16},{16,32},{32,48},{48,0},{1,17},{17,33},{33,49},{49,1},{2,18}... | collective-permute-start | bytes 105224 | tf_op jit(solution)/shard_map/ppermute | solution.py:536
  6.0 11.2 %collective-permute-start.2 = (f32[64,274]{1,0:T(8,128)S(1)}, f32[64,274]{1,0:T(8,128)S(1)}, u32[]{:S(2)}, u32[]{:S(2)}) collective-permute-start(f32[64,274]{1,0:T(8,128)S(1)} %bitcast.27), channel_id=1, source_target_pairs={{0,1},{1,2},{2,3},{3,4},{4,5},{5,6},{6,7},{7,8},{8,9},{9,10},{10,1... | collective-permute-start | bytes 210440 | tf_op jit(solution)/shard_map/ppermute | solution.py:536
  8.0 9.2 %collective-permute-start.3 = (f32[64,274]{1,0:T(8,128)S(1)}, f32[64,274]{1,0:T(8,128)S(1)}, u32[]{:S(2)}, u32[]{:S(2)}) collective-permute-start(f32[64,274]{1,0:T(8,128)S(1)} %bitcast.28), channel_id=1, source_target_pairs={{0,15},{1,0},{2,1},{3,2},{4,3},{5,4},{6,5},{7,6},{8,7},{9,8},{10,9... | collective-permute-start | bytes 210440 | tf_op jit(solution)/shard_map/ppermute | solution.py:536
  25.2 4.6 %collective-permute-start.4 = (f32[512,384]{1,0:T(8,128)S(1)}, f32[512,384]{1,0:T(8,128)S(1)}, u32[]{:S(2)}, u32[]{:S(2)}) collective-permute-start(f32[512,384]{1,0:T(8,128)S(1)} %get-tuple-element.41), channel_id=1, source_target_pairs={{0,64},{64,0},{1,65},{65,1},{2,66},{66,2},{3,67},{67,3},{4,68},{68... | collective-permute-start | bytes 2359304 | tf_op jit(solution)/shard_map/ppermute | solution.py:548
  60.8 10.7 %collective-permute-start.8 = (f32[64,274]{1,0:T(8,128)S(1)}, f32[64,274]{1,0:T(8,128)S(1)}, u32[]{:S(2)}, u32[]{:S(2)}) collective-permute-start(f32[64,274]{1,0:T(8,128)S(1)} %get-tuple-element.57), channel_id=1, source_target_pairs={{0,1},{1,2},{2,3},{3,4},{4,5},{5,6},{6,7},{7,8},{8,9},{9,10},{10,1... | collective-permute-start | bytes 210440 | tf_op jit(solution)/shard_map/ppermute | solution.py:536
  60.9 10.6 %collective-permute-start.9 = (f32[64,274]{1,0:T(8,128)S(1)}, f32[64,274]{1,0:T(8,128)S(1)}, u32[]{:S(2)}, u32[]{:S(2)}) collective-permute-start(f32[64,274]{1,0:T(8,128)S(1)} %get-tuple-element.58), channel_id=1, source_target_pairs={{0,15},{1,0},{2,1},{3,2},{4,3},{5,4},{6,5},{7,6},{8,7},{9,8},{10,9... | collective-permute-start | bytes 210440 | tf_op jit(solution)/shard_map/ppermute | solution.py:536
  66.2 5.3 %collective-permute-start.6 = (f32[1,32,274]{2,1,0:T(8,128)S(1)}, f32[1,32,274]{2,1,0:T(8,128)S(1)}, u32[]{:S(2)}, u32[]{:S(2)}) collective-permute-start(f32[1,32,274]{2,1,0:T(8,128)S(1)} %get-tuple-element.55), channel_id=1, source_target_pairs={{0,16},{16,32},{32,48},{48,0},{1,17},{17,33},{33,49},{49,1},{2,18}... | collective-permute-start | bytes 105224 | tf_op jit(solution)/shard_map/ppermute | solution.py:536
  66.2 5.3 %collective-permute-start.7 = (f32[1,32,274]{2,1,0:T(8,128)S(1)}, f32[1,32,274]{2,1,0:T(8,128)S(1)}, u32[]{:S(2)}, u32[]{:S(2)}) collective-permute-start(f32[1,32,274]{2,1,0:T(8,128)S(1)} %get-tuple-element.56), channel_id=1, source_target_pairs={{0,48},{16,0},{32,16},{48,32},{1,49},{17,1},{33,17},{49,33},{2,50}... | collective-permute-start | bytes 105224 | tf_op jit(solution)/shard_map/ppermute | solution.py:536
  77.6 10.8 %collective-permute-start.12 = (f32[64,274]{1,0:T(8,128)S(1)}, f32[64,274]{1,0:T(8,128)S(1)}, u32[]{:S(2)}, u32[]{:S(2)}) collective-permute-start(f32[64,274]{1,0:T(8,128)S(1)} %get-tuple-element.63), channel_id=1, source_target_pairs={{0,1},{1,2},{2,3},{3,4},{4,5},{5,6},{6,7},{7,8},{8,9},{9,10},{10,1... | collective-permute-start | bytes 210440 | tf_op jit(solution)/shard_map/ppermute | solution.py:536
  77.7 10.7 %collective-permute-start.13 = (f32[64,274]{1,0:T(8,128)S(1)}, f32[64,274]{1,0:T(8,128)S(1)}, u32[]{:S(2)}, u32[]{:S(2)}) collective-permute-start(f32[64,274]{1,0:T(8,128)S(1)} %get-tuple-element.64), channel_id=1, source_target_pairs={{0,15},{1,0},{2,1},{3,2},{4,3},{5,4},{6,5},{7,6},{8,7},{9,8},{10,9... | collective-permute-start | bytes 210440 | tf_op jit(solution)/shard_map/ppermute | solution.py:536
  83.0 5.3 %collective-permute-start.10 = (f32[1,32,274]{2,1,0:T(8,128)S(1)}, f32[1,32,274]{2,1,0:T(8,128)S(1)}, u32[]{:S(2)}, u32[]{:S(2)}) collective-permute-start(f32[1,32,274]{2,1,0:T(8,128)S(1)} %get-tuple-element.61), channel_id=1, source_target_pairs={{0,16},{16,32},{32,48},{48,0},{1,17},{17,33},{33,49},{49,1},{2,18}... | collective-permute-start | bytes 105224 | tf_op jit(solution)/shard_map/ppermute | solution.py:536
  120.5 19.9 %collective-permute-start.15 = (f32[512,384]{1,0:T(8,128)S(1)}, f32[512,384]{1,0:T(8,128)S(1)}, u32[]{:S(2)}, u32[]{:S(2)}) collective-permute-start(f32[512,384]{1,0:T(8,128)S(1)} %get-tuple-element.71), channel_id=1, source_target_pairs={{0,64},{64,0},{1,65},{65,1},{2,66},{66,2},{3,67},{67,3},{4,68},{68... | collective-permute-start | bytes 2359304 | tf_op jit(solution)/shard_map/ppermute | solution.py:548
  125.9 5.1 %collective-permute-start.22 = (f32[8,128]{1,0:T(8,128)S(1)}, f32[8,128]{1,0:T(8,128)S(1)}, u32[]{:S(2)}, u32[]{:S(2)}) collective-permute-start(f32[8,128]{1,0:T(8,128)S(1)} %add.86), channel_id=1, source_target_pairs={{0,32},{16,48},{32,0},{48,16},{1,33},{17,49},{33,1},{49,17},{2,34}... | collective-permute-start | bytes 12296 | tf_op jit(solution)/shard_map/ppermute | solution.py:536
  125.9 5.1 %collective-permute-start.21 = (f32[8,128]{1,0:T(8,128)S(1)}, f32[8,128]{1,0:T(8,128)S(1)}, u32[]{:S(2)}, u32[]{:S(2)}) collective-permute-start(f32[8,128]{1,0:T(8,128)S(1)} %add.86), channel_id=1, source_target_pairs={{0,16},{16,32},{32,48},{48,0},{1,17},{17,33},{33,49},{49,1},{2,18}... | collective-permute-start | bytes 12296 | tf_op jit(solution)/shard_map/ppermute | solution.py:536
  131.1 5.2 %collective-permute-start.25 = (f32[8,128]{1,0:T(8,128)S(1)}, f32[8,128]{1,0:T(8,128)S(1)}, u32[]{:S(2)}, u32[]{:S(2)}) collective-permute-start(f32[8,128]{1,0:T(8,128)S(1)} %add_add_fusion.2), channel_id=1, source_target_pairs={{0,2},{1,3},{2,0},{3,1},{4,6},{5,7},{6,4},{7,5},{8,10},{9,11},{10,... | collective-permute-start | bytes 12296 | tf_op jit(solution)/shard_map/ppermute | solution.py:563
  131.2 6.2 %collective-permute-start.24 = (f32[8,128]{1,0:T(8,128)S(1)}, f32[8,128]{1,0:T(8,128)S(1)}, u32[]{:S(2)}, u32[]{:S(2)}) collective-permute-start(f32[8,128]{1,0:T(8,128)S(1)} %add_add_fusion.2), channel_id=1, source_target_pairs={{0,1},{1,2},{2,3},{3,0},{4,5},{5,6},{6,7},{7,4},{8,9},{9,10},{10,1... | collective-permute-start | bytes 12296 | tf_op jit(solution)/shard_map/ppermute | solution.py:563
  137.4 11.2 %collective-permute-start.29 = (f32[8,128]{1,0:T(8,128)S(1)}, f32[8,128]{1,0:T(8,128)S(1)}, u32[]{:S(2)}, u32[]{:S(2)}) collective-permute-start(f32[8,128]{1,0:T(8,128)S(1)} %add_add_fusion.1), channel_id=1, source_target_pairs={{0,12},{1,13},{2,14},{3,15},{4,0},{5,1},{6,2},{7,3},{8,4},{9,5},{1... | collective-permute-start | bytes 12296 | tf_op jit(solution)/shard_map/ppermute | solution.py:563
  139.4 9.2 %collective-permute-start.28 = (f32[8,128]{1,0:T(8,128)S(1)}, f32[8,128]{1,0:T(8,128)S(1)}, u32[]{:S(2)}, u32[]{:S(2)}) collective-permute-start(f32[8,128]{1,0:T(8,128)S(1)} %add_add_fusion.1), channel_id=1, source_target_pairs={{0,8},{1,9},{2,10},{3,11},{4,12},{5,13},{6,14},{7,15},{8,0},{9,1},... | collective-permute-start | bytes 12296 | tf_op jit(solution)/shard_map/ppermute | solution.py:563
  139.4 14.6 %collective-permute-start.27 = (f32[8,128]{1,0:T(8,128)S(1)}, f32[8,128]{1,0:T(8,128)S(1)}, u32[]{:S(2)}, u32[]{:S(2)}) collective-permute-start(f32[8,128]{1,0:T(8,128)S(1)} %add_add_fusion.1), channel_id=1, source_target_pairs={{0,4},{1,5},{2,6},{3,7},{4,8},{5,9},{6,10},{7,11},{8,12},{9,13},{1... | collective-permute-start | bytes 12296 | tf_op jit(solution)/shard_map/ppermute | solution.py:563
  145.3 8.7 %collective-permute-start.16 = (f32[1,32,274]{2,1,0:T(8,128)S(1)}, f32[1,32,274]{2,1,0:T(8,128)S(1)}, u32[]{:S(2)}, u32[]{:S(2)}) collective-permute-start(f32[1,32,274]{2,1,0:T(8,128)S(1)} %get-tuple-element.73), channel_id=1, source_target_pairs={{0,16},{16,32},{32,48},{48,0},{1,17},{17,33},{33,49},{49,1},{2,18}... | collective-permute-start | bytes 105224 | tf_op jit(solution)/shard_map/ppermute | solution.py:536
  145.4 8.6 %collective-permute-start.17 = (f32[1,32,274]{2,1,0:T(8,128)S(1)}, f32[1,32,274]{2,1,0:T(8,128)S(1)}, u32[]{:S(2)}, u32[]{:S(2)}) collective-permute-start(f32[1,32,274]{2,1,0:T(8,128)S(1)} %get-tuple-element.74), channel_id=1, source_target_pairs={{0,48},{16,0},{32,16},{48,32},{1,49},{17,1},{33,17},{49,33},{2,50}... | collective-permute-start | bytes 105224 | tf_op jit(solution)/shard_map/ppermute | solution.py:536
  148.6 7.9 %collective-permute-start.18 = (f32[64,274]{1,0:T(8,128)S(1)}, f32[64,274]{1,0:T(8,128)S(1)}, u32[]{:S(2)}, u32[]{:S(2)}) collective-permute-start(f32[64,274]{1,0:T(8,128)S(1)} %get-tuple-element.75), channel_id=1, source_target_pairs={{0,1},{1,2},{2,3},{3,4},{4,5},{5,6},{6,7},{7,8},{8,9},{9,10},{10,1... | collective-permute-start | bytes 210440 | tf_op jit(solution)/shard_map/ppermute | solution.py:536
  148.6 7.9 %collective-permute-start.19 = (f32[64,274]{1,0:T(8,128)S(1)}, f32[64,274]{1,0:T(8,128)S(1)}, u32[]{:S(2)}, u32[]{:S(2)}) collective-permute-start(f32[64,274]{1,0:T(8,128)S(1)} %get-tuple-element.76), channel_id=1, source_target_pairs={{0,15},{1,0},{2,1},{3,2},{4,3},{5,4},{6,5},{7,6},{8,7},{9,8},{10,9... | collective-permute-start | bytes 210440 | tf_op jit(solution)/shard_map/ppermute | solution.py:536
  (34 other events, 295.4 us)
where the time goes:
time: 165 us; the launch traced here: 164 us
  Pallas kernels  86.2 us (52%)
  starting transfers between devices  45.9 us (28%)
  waiting for transfers between devices  20.5 us (12%)
  local copies, waits for them, and re-layouts  8.78 us (5%)
    ppermute x19, starting transfers between devices, shifted(): lax.ppermute(value, axis, [(i, (i + step) % count) for i in range(count)])  39.4 us
    pallas_call x2, Pallas kernels, forward_call(): call(functools.partial(forward_kernel, with_sums), out, [smem] + [vmem] *...  26.9 us
    pallas_call x2, Pallas kernels, backward_call(): call(functools.partial(backward_kernel, scale), [shape((rows, WIDE))] * 2...  19.9 us
    pallas_call x2, Pallas kernels, tangent_call(): call(functools.partial(tangent_kernel, with_square), out, [smem, smem] +...  12.2 us
    ppermute x19, waiting for transfers between devices, shifted(): lax.ppermute(value, axis, [(i, (i + step) % count) for i in range(count)])  11 us
    pallas_call x2, Pallas kernels, spread_call(): call(spread_kernel, out, [smem] + [vmem] * 5, [vmem] * 5, [pltpu.VMEM((2,...  9.89 us
    pallas_call x1, Pallas kernels, final_call(): call(final_kernel, [shape(field.shape)] * 2, [vmem] * 10, [hbm] * 2, [plt...  6.9 us
    pallas_call x1, Pallas kernels, basis_call(): call(basis_kernel, out, [vmem] * 9, [vmem] * 6, [], 6, 4)  6.07 us
  transfers between devices with their start and end apart: 30, of which 12 were waited for; matrix products, arithmetic and copies ran while one was open for 4% of the time, Pallas kernels for 6%

commit v1 on v0

--- a/solution.py
+++ b/solution.py
@@ -212,7 +212,7 @@
 
 
 def tangent_call(with_square, cells, counts, field, halo, coupling, rates):
-    lats, lons, width = field.shape
+    lats, lons, _ = field.shape
     slots = cells.shape[1]
     out = [shape((slots, WIDE))] * 2 + [shape((8, 128))] * with_square
     return call(
@@ -239,12 +239,18 @@
     return dot(upper, pick[0]) + dot(upper, pick[1]) + dot(lo[...], pick[0])
 
 
-def layer(left, right, columns, transposed, finish, carry=0):
+def layer(left, right, columns, transposed, finish, held, carry=0):
+    steps = columns // BLOCK
+
     def body(k, carry):
-        n = pl.multiple_of(k * BLOCK, BLOCK)
-        return finish(n, tile(left, right, n, transposed), carry)
-
-    return lax.fori_loop(0, columns // BLOCK, body, carry)
+        value = tile(left, right, pl.multiple_of(k * BLOCK, BLOCK), transposed)
+        n = pl.multiple_of(jnp.maximum(k - 1, 0) * BLOCK, BLOCK)
+        after = finish(n, held[...], carry)
+        held[...] = value
+        return jax.tree.map(lambda new, old: jnp.where(k > 0, new, old), after, carry)
+
+    carry = lax.fori_loop(0, steps, body, carry)
+    return finish((steps - 1) * BLOCK, held[...], carry)
 
 
 def gated(gate, target):
@@ -265,7 +271,7 @@
         sums_in, z_hi, z_lo, sums = rest[:4]
     else:
         z_hi, z_lo = rest[:2]
-    x_hi, x_lo, a_hi, a_lo, b_hi, b_lo, t_full, t_hi, t_lo = rest[-9:]
+    x_hi, x_lo, a_hi, a_lo, b_hi, b_lo, t_full, t_hi, t_lo, held = rest[-10:]
     rows = own.shape[0]
     for start, part in ((0, own), (WIDE, other)):
         upper, lower = halves_of(part[...])
@@ -273,8 +279,8 @@
         x_lo[:, start : start + WIDE] = lower
     hidden = mid_hi.shape[0]
     channels = cov_hi.shape[0]
-    layer((x_hi, x_lo), (in_hi, in_lo), hidden, False, gated(gate_one, (a_hi, a_lo)))
-    layer((a_hi, a_lo), (mid_hi, mid_lo), hidden, False, gated(gate_two, (b_hi, b_lo)))
+    layer((x_hi, x_lo), (in_hi, in_lo), hidden, False, gated(gate_one, (a_hi, a_lo)), held)
+    layer((a_hi, a_lo), (mid_hi, mid_lo), hidden, False, gated(gate_two, (b_hi, b_lo)), held)
 
     def keep_outputs(n, value, carry):
         if with_sums:
@@ -284,7 +290,7 @@
         t_lo[:, pl.ds(n, BLOCK)] = lower
         return carry
 
-    layer((b_hi, b_lo), (out_hi, out_lo), channels, True, keep_outputs)
+    layer((b_hi, b_lo), (out_hi, out_lo), channels, True, keep_outputs, held)
     live = lax.broadcasted_iota(jnp.int32, (rows, BLOCK), 0) < counts[0]
 
     def keep_weighted(n, value, carry):
@@ -296,19 +302,21 @@
         return carry
 
     total = jnp.zeros((8, BLOCK), f32)
-    total = layer((t_hi, t_lo), (cov_hi, cov_lo), channels, False, keep_weighted, total)
+    total = layer((t_hi, t_lo), (cov_hi, cov_lo), channels, False, keep_weighted, held, total)
     if with_sums:
         lane = lax.broadcasted_iota(jnp.int32, (8, 128), 1)
         sums[...] = jnp.where(lane == 3, jnp.sum(total), sums_in[...])
 
 
 def backward_kernel(
-    scale, z_hi, z_lo, gate_one, gate_two, in_hi, in_lo, mid_hi, mid_lo, out_hi, out_lo,
-    own_grad, other_grad, a_hi, a_lo, b_hi, b_lo
+    z_hi, z_lo, gate_one, gate_two, mid_hi, mid_lo, out_hi, out_lo, b_hi, b_lo, a_hi, a_lo, held
 ):
     hidden = mid_hi.shape[0]
-    layer((z_hi, z_lo), (out_hi, out_lo), hidden, False, gated(gate_two, (a_hi, a_lo)))
-    layer((a_hi, a_lo), (mid_hi, mid_lo), hidden, True, gated(gate_one, (b_hi, b_lo)))
+    layer((z_hi, z_lo), (out_hi, out_lo), hidden, False, gated(gate_two, (a_hi, a_lo)), held)
+    layer((a_hi, a_lo), (mid_hi, mid_lo), hidden, True, gated(gate_one, (b_hi, b_lo)), held)
+
+
+def gradient_kernel(scale, b_hi, b_lo, in_hi, in_lo, own_grad, other_grad):
     for start in range(0, 2 * WIDE, BLOCK):
         value = tile((b_hi, b_lo), (in_hi, in_lo), start, True)
         for first, target in ((0, own_grad), (WIDE, other_grad)):
@@ -333,36 +341,107 @@
         + pair(hidden)
         + pair(hidden)
         + [pltpu.VMEM((rows, channels), f32)]
-        + pair(channels),
+        + pair(channels)
+        + [pltpu.VMEM((rows, BLOCK), f32)],
         16,
         13,
     )(*args)
 
 
-def backward_call(scale, z, gates, weights):
+def backward_call(z, gates, weights):
     rows = z[0].shape[0]
     hidden = weights[2].shape[0]
-    args = (*z, *gates, *weights[:6])
+    args = (*z, *gates, *weights[2:6])
     return call(
-        functools.partial(backward_kernel, scale),
-        [shape((rows, WIDE))] * 2,
+        backward_kernel,
+        [shape((rows, hidden), bf16)] * 2,
         [vmem] * len(args),
         [vmem] * 2,
-        [pltpu.VMEM((rows, hidden), bf16)] * 4,
+        [pltpu.VMEM((rows, hidden), bf16)] * 2 + [pltpu.VMEM((rows, BLOCK), f32)],
         10,
-        11,
+        8,
     )(*args)
 
 
-def spread_kernel(counts, cells, own, other, coupling, edge, field, south, north, west, east, parts):
-    lats, lons, width = field.shape
+def gradient_call(scale, back, weights):
+    rows = back[0].shape[0]
+    return call(
+        functools.partial(gradient_kernel, scale),
+        [shape((rows, WIDE))] * 2,
+        [vmem] * 4,
+        [vmem] * 2,
+        [],
+        8,
+        3,
+    )(*back, *weights[:2])
+
+
+def hot_rows(cell, cells):
+    return (cell == cells).astype(f32).astype(bf16)
+
+
+def merged(both):
+    return both[:, :WIDE] + both[:, WIDE:]
+
+
+def edge_kernel(
+    counts, cells, own, other, coupling, columns, parts, south, north, west, east, *lines
+):
+    lats, lons, _ = coupling.shape
     slots = own.shape[0]
-    chunk = 512
+    width = west.shape[1]
     for k, part in enumerate((own, other)):
         row = lax.broadcasted_iota(jnp.int32, (slots, WIDE), 0)
         upper, lower = halves_of(jnp.where(row < counts[k], part[...], 0.0))
         parts[k, :, 0:WIDE] = upper
         parts[k, :, WIDE : 2 * WIDE] = lower
+    total = 4 * lats + 4 * lons
+    r = lax.broadcasted_iota(jnp.int32, (total, BLOCK), 0)
+    cell = jnp.full_like(r, -1)
+    start = 0
+    spans = []
+    for lon in (0, 1, lons - 2, lons - 1):
+        inside = (r >= start) & (r < start + lats)
+        cell = jnp.where(inside, (r - start) * lons + lon, cell)
+        spans.append((start, lats))
+        start += lats
+    for lat in (0, 1, lats - 2, lats - 1):
+        inside = (r >= start) & (r < start + lons)
+        cell = jnp.where(inside, r - start + lat * lons, cell)
+        spans.append((start, lons))
+        start += lons
+    value = jnp.zeros((total, 2 * WIDE), f32)
+    for k in range(2):
+        for s in range(0, slots, BLOCK):
+            hot = hot_rows(cell, cells[k : k + 1, s : s + BLOCK])
+            value = value + jnp.dot(hot, parts[k, s : s + BLOCK, :], preferred_element_type=f32)
+    value = merged(value)[:, :width]
+    for line, (start, count) in zip(lines, spans):
+        line[...] = value[start : start + count]
+    west[...] = lines[0][...] * columns[:, 1:2]
+    east[...] = lines[3][...] * columns[:, 0:1]
+    south[0] = lines[4][...] * coupling[0][:, 3:4]
+    north[0] = lines[7][...] * coupling[lats - 1][:, 2:3]
+
+
+def edge_shapes(lats, lons, width):
+    return [shape((1, lons, width))] * 2 + [shape((lats, width))] * 2
+
+
+def edge_call(counts, cells, own, other, coupling, columns, width):
+    lats, lons, _ = coupling.shape
+    slots = own.shape[0]
+    out = [shape((2, slots, 2 * WIDE), bf16)] + edge_shapes(lats, lons, width)
+    out += [shape((lats, width))] * 4 + [shape((lons, width))] * 4
+    return call(edge_kernel, out, [smem] + [vmem] * 5, [vmem] * len(out), [], 12, 2)(
+        counts, cells, own, other, coupling, columns
+    )
+
+
+def spread_kernel(counts, cells, parts, field):
+    lats, lons, width = field.shape
+    slots = parts.shape[1]
+    chunk = 512
 
     def body(b, carry):
         first = b * chunk
@@ -370,10 +449,9 @@
         lat = pl.ds(b * (chunk // lons), chunk // lons)
 
         def piece(k, s):
-            hot = (cell == cells[k : k + 1, s : s + BLOCK]).astype(f32).astype(bf16)
+            hot = hot_rows(cell, cells[k : k + 1, s : s + BLOCK])
             both = jnp.dot(hot, parts[k, s : s + BLOCK, :], preferred_element_type=f32)
-            total = both[:, :WIDE] + both[:, WIDE:]
-            return total[:, :width].reshape(chunk // lons, lons, width)
+            return merged(both)[:, :width].reshape(chunk // lons, lons, width)
 
         field[lat] = piece(0, 0) + piece(1, 0)
         for k in range(2):
@@ -387,38 +465,57 @@
 
     lax.fori_loop(0, lats * lons // chunk, body, 0)
 
-    def move(b, carry):
-        for k in range(8):
-            i = b * 8 + k
-            value = field[i]
-            west[pl.ds(i, 1), :] = value[:1]
-            east[pl.ds(i, 1), :] = value[lons - 1 :]
-        return carry
-
-    lax.fori_loop(0, lats // 8, move, 0)
-    east[...] = east[...] * edge[:, 0:1]
-    west[...] = west[...] * edge[:, 1:2]
-    south[0] = field[0] * coupling[0][:, 3:4]
-    north[0] = field[lats - 1] * coupling[lats - 1][:, 2:3]
-
-
-def edge_shapes(lats, lons, width):
-    return [shape((1, lons, width))] * 2 + [shape((lats, width))] * 2
-
-
-def spread_call(counts, cells, own, other, coupling, edge, width):
-    lats, lons, _ = coupling.shape
-    slots = own.shape[0]
-    out = [shape((lats, lons, width))] + edge_shapes(lats, lons, width)
+
+def spread_call(counts, cells, parts, lats, lons, width):
     return call(
         spread_kernel,
-        out,
-        [smem] + [vmem] * 5,
-        [vmem] * 5,
-        [pltpu.VMEM((2, slots, 2 * WIDE), bf16)],
-        10,
-        5,
-    )(counts, cells, own, other, coupling, edge)
+        [shape((lats, lons, width))],
+        [smem] + [vmem] * 2,
+        [vmem],
+        [],
+        8,
+        4,
+    )(counts, cells, parts)[0]
+
+
+def border_kernel(
+    south, north, west, east, w0, w1, e1, e0, s0, s1, n1, n0, coupling, columns, rates,
+    out_south, out_north, out_west, out_east
+):
+    lats, width = w0.shape
+    lons = s0.shape[0]
+    rate = rates[...]
+    lat = lax.broadcasted_iota(jnp.int32, (lats, width), 0)
+    lon = lax.broadcasted_iota(jnp.int32, (lons, width), 0)
+
+    def column(line, inner, halo, first, target, end):
+        c = [columns[:, first + k : first + k + 1] for k in range(4)]
+        value = line[...]
+        flux = halo[...] + c[0] * inner[...]
+        flux = flux + from_west(c[1] * value, south[0, end : end + 1, :], lat)
+        flux = flux + from_east(c[2] * value, north[0, end : end + 1, :], lat)
+        target[...] = value + rate * (flux - c[3] * value)
+
+    column(w0, w1, west, 2, out_west, 0)
+    column(e0, e1, east, 6, out_east, lons - 1)
+
+    def along(i, line, flux):
+        c = coupling[i]
+        value = line[...]
+        flux = flux + from_west(c[:, 0:1] * value, west[i : i + 1, :], lon)
+        flux = flux + from_east(c[:, 1:2] * value, east[i : i + 1, :], lon)
+        return value + rate * (flux - c[:, 4:5] * value)
+
+    out_south[0] = along(0, s0, south[0] + coupling[1][:, 3:4] * s1[...])
+    out_north[0] = along(lats - 1, n0, north[0] + coupling[lats - 2][:, 2:3] * n1[...])
+
+
+def border_call(halo, lines, coupling, columns, rates):
+    lats, width = lines[0].shape
+    out = edge_shapes(lats, lines[4].shape[0], width)
+    return call(border_kernel, out, [vmem] * 15, [vmem] * 4, [], 4, 1)(
+        *halo, *lines, coupling, columns, rates
+    )
 
 
 def adjoint_rows(field, south, north, west, east, coupling, rates, finish, carry, after=None):
@@ -432,8 +529,7 @@
         flux = below + above
         flux = flux + from_west(c[:, 0:1] * value, west[pl.ds(i, 1), :], lon)
         flux = flux + from_east(c[:, 1:2] * value, east[pl.ds(i, 1), :], lon)
-        total = c[:, 0:1] + c[:, 1:2] + c[:, 2:3] + c[:, 3:4]
-        return finish(i, value + rate * (flux - total * value), carry)
+        return finish(i, value + rate * (flux - c[:, 4:5] * value), carry)
 
     def below(i):
         return coupling[i - 1][:, 2:3] * field[i - 1]
@@ -445,32 +541,26 @@
 
 
 def basis_kernel(
-    field, south, north, west, east, coupling, rates, right_side, sums_in,
-    basis, out_south, out_north, out_west, out_east, sums
-):
-    lats, lons, width = field.shape
+    field, south, north, west, east, coupling, rates, right_side, sums_in, basis, sums
+):
+    _, _, width = field.shape
 
     def finish(i, value, carry):
         basis[i] = value
-        out_west[pl.ds(i, 1), :] = value[:1]
-        out_east[pl.ds(i, 1), :] = value[lons - 1 :]
         return carry[0] + folded(right_side[i] * value), carry[1] + folded(value * value)
 
     zero = jnp.zeros((8, width), f32)
     cross, square = adjoint_rows(
         field, south, north, west, east, coupling, rates, finish, (zero, zero)
     )
-    out_south[0] = basis[0]
-    out_north[0] = basis[lats - 1]
     lane = lax.broadcasted_iota(jnp.int32, (8, 128), 1)
     result = jnp.where(lane == 1, jnp.sum(cross), sums_in[...])
     sums[...] = jnp.where(lane == 2, jnp.sum(square), result)
 
 
 def basis_call(field, halo, coupling, rates, right_side, sums):
-    lats, lons, width = field.shape
-    out = [shape((lats, lons, width))] + edge_shapes(lats, lons, width) + [shape((8, 128))]
-    return call(basis_kernel, out, [vmem] * 9, [vmem] * 6, [], 6, 4)(
+    out = [shape(field.shape), shape((8, 128))]
+    return call(basis_kernel, out, [vmem] * 9, [vmem] * 2, [], 6, 5)(
         field, *halo, coupling, rates, right_side, sums
     )
 
@@ -479,7 +569,7 @@
     field, south, north, west, east, coupling, rates, right_side, basis, sums,
     solution_out, residual_out, solution_part, residual_part, sems
 ):
-    lats, lons, width = field.shape
+    lats, _, _ = field.shape
     s = sums[0:1, :]
     rr, rv, vv, vy = s[:, 0:1], s[:, 1:2], s[:, 2:3], s[:, 3:4]
     q = SCALE * rv
@@ -593,8 +683,11 @@
         jnp.where(north_open, couplings[2], 0.0),
         jnp.where(south_open, couplings[3], 0.0),
     ]
+    planes.append(planes[0] + planes[1] + planes[2] + planes[3])
     coupling = jnp.stack(planes, axis=2)
-    edge = jnp.stack([couplings[0, :, lons - 1], couplings[1, :, 0]], axis=1)
+    pick = ((0, lons - 1), (1, 0), (1, 1), (2, 0), (3, 0), (4, 0))
+    pick += ((0, lons - 2), (2, lons - 1), (3, lons - 1), (4, lons - 1))
+    columns = jnp.stack([planes[k][:, j] for k, j in pick], axis=1)
     rates = channel_rates[None, :]
     order = jnp.stack([side_index, 1 - side_index])
     cells = jnp.clip(profile_cells[order], 0, lats * lons - 1)
@@ -606,17 +699,24 @@
 
     own, other, sums = tangent_call(True, cells, counts, right_side, halo, coupling, rates)
     z = forward_call(counts, own, swapped(other), gates, weights, None)
-    own, other = backward_call(1.0 / SCALE, z, gates, weights)
-    field, *out = spread_call(counts, cells, own, swapped(other), coupling, edge, width)
-    halo = exchanged(*out)
-    basis, *out, sums = basis_call(field, halo, coupling, rates, right_side, sums)
-    halo = exchanged(*out)
-    own, other = tangent_call(False, cells, counts, basis, halo, coupling, rates)
+    back = backward_call(z, gates, weights)
+    own, other = gradient_call(1.0 / SCALE, back, weights)
+    other = swapped(other)
+    parts, *out = edge_call(counts, cells, own, other, coupling, columns, width)
+    halo = exchanged(*out[:4])
+    field = spread_call(counts, cells, parts, lats, lons, width)
+    outer = border_call(halo, out[4:], coupling, columns, rates)
+    outer = exchanged(*outer)
+    basis, sums = basis_call(field, halo, coupling, rates, right_side, sums)
+    own, other = tangent_call(False, cells, counts, basis, outer, coupling, rates)
     *z, sums = forward_call(counts, own, swapped(other), gates, weights, sums)
     sums = everyone(sums)
-    own, other = backward_call(1.0, z, gates, weights)
-    field, *out = spread_call(counts, cells, own, swapped(other), coupling, edge, width)
-    halo = exchanged(*out)
+    back = backward_call(z, gates, weights)
+    own, other = gradient_call(1.0, back, weights)
+    other = swapped(other)
+    parts, *out = edge_call(counts, cells, own, other, coupling, columns, width)
+    halo = exchanged(*out[:4])
+    field = spread_call(counts, cells, parts, lats, lons, width)
     return tuple(final_call(field, halo, coupling, rates, right_side, basis, sums))
 
 

time: 165 us -> 159 us (0.964)
  Pallas kernels: 86.2 us -> 80.5 us
  waiting for transfers between devices: 20.5 us -> 18.8 us
    ppermute x19, waiting for transfers between devices: 11 us -> 4.29 us  [shifted(): lax.ppermute(value, axis, [(i, (i + step) % count) for i in range(count)])]
    ppermute x6, waiting for transfers between devices: 4.26 us -> 8.67 us  [everyone(): total = total + lax.ppermute(base, 'col', pairs)]
    pallas_call x2, Pallas kernels: 12.2 us -> 9.4 us  [tangent_call(): call(functools.partial(tangent_kernel, with_square), out, [smem, smem] +...]
    ppermute x6, starting transfers between devices: 5.05 us -> 7.45 us  [everyone(): total = total + lax.ppermute(base, 'col', pairs)]
    pallas_call x5 -> x10, Pallas kernels: 35.8 us -> 33.9 us  [the longest x2 15 us: backward_call(): call(backward_kernel, [shape((rows, hidden), bf16)] * 2, [vmem] * len(arg...]
    ppermute x19, starting transfers between devices: 39.4 us -> 37.5 us  [shifted(): lax.ppermute(value, axis, [(i, (i + step) % count) for i in range(count)])]
    pallas_call x1, Pallas kernels: 6.9 us -> 5.23 us  [final_call(): call(final_kernel, [shape(field.shape)] * 2, [vmem] * 10, [hbm] * 2, [plt...]
    unnamed x58 -> x64, local copies, waits for them, and re-layouts: 2.03 us -> 3.49 us
  transfers between devices with their start and end apart: 30 -> 30, of which waited for: 12 -> 11; matrix products, arithmetic and copies ran while one was open for 4% -> 5% of each run, Pallas kernels for 6% -> 9%
where the time goes in v1:
time: 159 us; the launch traced here: 158 us
  Pallas kernels  80.5 us (51%)
  starting transfers between devices  46.4 us (29%)
  waiting for transfers between devices  18.8 us (12%)
  local copies, waits for them, and re-layouts  8.87 us (6%)
  other arithmetic  2.35 us (1%)
    ppermute x19, starting transfers between devices, shifted(): lax.ppermute(value, axis, [(i, (i + step) % count) for i in range(count)])  37.5 us
    pallas_call x2, Pallas kernels, forward_call(): call(functools.partial(forward_kernel, with_sums), out, [smem] + [vmem] *...  27.7 us
    pallas_call x2, Pallas kernels, backward_call(): call(backward_kernel, [shape((rows, hidden), bf16)] * 2, [vmem] * len(arg...  15 us
    pallas_call x2, Pallas kernels, tangent_call(): call(functools.partial(tangent_kernel, with_square), out, [smem, smem] +...  9.4 us
    ppermute x6, waiting for transfers between devices, everyone(): total = total + lax.ppermute(base, 'col', pairs)  8.67 us
    ppermute x6, starting transfers between devices, everyone(): total = total + lax.ppermute(base, 'col', pairs)  7.45 us
    ppermute x5, waiting for transfers between devices, swapped(): return lax.ppermute(value, 'side', [(0, 1), (1, 0)])  5.8 us
    pallas_call x2, Pallas kernels, spread_call(): call(spread_kernel, [shape((lats, lons, width))], [smem] + [vmem] * 2, [v...  5.78 us
  transfers between devices with their start and end apart: 30, of which 11 were waited for; matrix products, arithmetic and copies ran while one was open for 5% of the time, Pallas kernels for 9%

profile of v1, /device:TPU:0, one launch (start us, length us, event | category | flops | bytes accessed | tf_op | source)
XLA Modules:
  0.0 158.5 jit_solution(10106497492838155184)
XLA Ops:
  1.5 2.9 %collective-permute-start.1 = (f32[1,32,274]{2,1,0:T(8,128)S(1)}, f32[1,32,274]{2,1,0:T(8,128)S(1)}, u32[]{:S(2)}, u32[]{:S(2)}) collective-permute-start(f32[1,32,274]{2,1,0:T(8,128)S(1)} %get-tuple-element.107), channel_id=1, source_target_pairs={{0,48},{16,0},{32,16},{48,32},{1,49},{17,1},{33,17},{49,33},{2,50}... | collective-permute-start | bytes 105224 | tf_op jit(solution)/shard_map/ppermute | solution.py:626
  8.0 4.7 %collective-permute-start.3 = (f32[64,274]{1,0:T(8,128)S(1)}, f32[64,274]{1,0:T(8,128)S(1)}, u32[]{:S(2)}, u32[]{:S(2)}) collective-permute-start(f32[64,274]{1,0:T(8,128)S(1)} %bitcast.54), channel_id=1, source_target_pairs={{0,15},{1,0},{2,1},{3,2},{4,3},{5,4},{6,5},{7,6},{8,7},{9,8},{10,9... | collective-permute-start | bytes 210440 | tf_op jit(solution)/shard_map/ppermute | solution.py:626
  21.2 4.7 %shard_map.122 = (f32[512,384]{1,0:T(8,128)S(1)}, f32[512,384]{1,0:T(8,128)S(1)}, f32[8,128]{1,0:T(8,128)S(1)}) custom-call(s32[2,512]{1,0:T(2,128)S(1)} %broadcast_clamp_fusion.cells, s32[2]{0:T(128)S(1)} %gather_fusion, f32[64,32,274]{2,1,0:T(8,128)S(1)} %copy-done.2, f32[1,32,274]{2,1,0:T(8,128)S(1)} %collective-permute-done.south, ...), custom_call_target="tpu_custom_call" | custom-call | flops 6000000000 | bytes 18000000 | tf_op jit(solution)/shard_map/pallas_call | solution.py:218
  26.2 4.4 %shard_map.123 = (bf16[768,1024]{1,0:T(8,128)(2,1)S(1)}, bf16[768,1024]{1,0:T(8,128)(2,1)S(1)}, bf16[1024,1024]{1,0:T(8,128)(2,1)S(1)}, bf16[1024,1024]{1,0:T(8,...) custom-call(s32[1]{0:T(128)} %bitcast.10.side, ...), custom_call_target="tpu_custom_call" | custom-call | flops 5000000000 | bytes 15000000 | tf_op jit(solution)/shard_map/pallas_call | solution.py:152
  30.7 13.7 %shard_map.124 = (bf16[512,768]{1,0:T(8,128)(2,1)S(1)}, bf16[512,768]{1,0:T(8,128)(2,1)S(1)}) custom-call(s32[2]{0:T(128)S(1)} %gather_fusion, f32[512,384]{1,0:T(8,128)S(1)} %get-tuple-element.52.own, f32[512,384]{1,0:T(8,128)S(1)} %collective-permute-done.4.other, bf16[512,1024]{1,0:T(8,128)(2,1)S(1)} %copy-done.8, bf16[512,1024]{1,0:T(8,128)(2,1)S(1)} %copy-done.10, ...), custom_call_target="tpu_custom_call" | custom-call | flops 12999999488 | bytes 39000000 | tf_op jit(solution)/shard_map/pallas_call | solution.py:335
  44.4 7.5 %shard_map.125 = (bf16[512,1024]{1,0:T(8,128)(2,1)S(1)}, bf16[512,1024]{1,0:T(8,128)(2,1)S(1)}) custom-call(bf16[512,768]{1,0:T(8,128)(2,1)S(1)} %get-tuple-element.62.z_hi, bf16[512,768]{1,0:T(8,128)(2,1)S(1)} %get-tuple-element.63.z_lo, bf16[512,1024]{1,0:T(8,128)(2,1)S(1)} %copy-done.8, bf16[512,1024]{1,0:T(8,128)(2,1)S(1)} %copy-done.10, ...), custom_call_target="tpu_custom_call" | custom-call | flops 8000000000 | bytes 24000000 | tf_op jit(solution)/shard_map/pallas_call | solution.py:355
  52.0 2.6 %shard_map.126 = (f32[512,384]{1,0:T(8,128)S(1)}, f32[512,384]{1,0:T(8,128)S(1)}) custom-call(bf16[512,1024]{1,0:T(8,128)(2,1)S(1)} %get-tuple-element.64.b_hi, bf16[512,1024]{1,0:T(8,128)(2,1)S(1)} %get-tuple-element.65.b_lo, bf16[768,1024]{1,0:T(8,128)(2,1)S(1)} %get-tuple-element.54.in_hi, bf16[768,1024]{1,0:T(8,128)(2,1)S(1)} %get-tuple-element.55.in_lo), custom_call_target="tpu_custom_call" | custom-call | flops 3000000000 | bytes 9000000 | tf_op jit(solution)/shard_map/pallas_call | solution.py:368
  59.1 3.0 %collective-permute-start.7 = (f32[1,32,274]{2,1,0:T(8,128)S(1)}, f32[1,32,274]{2,1,0:T(8,128)S(1)}, u32[]{:S(2)}, u32[]{:S(2)}) collective-permute-start(f32[1,32,274]{2,1,0:T(8,128)S(1)} %get-tuple-element.70), channel_id=1, source_target_pairs={{0,48},{16,0},{32,16},{48,32},{1,49},{17,1},{33,17},{49,33},{2,50}... | collective-permute-start | bytes 105224 | tf_op jit(solution)/shard_map/ppermute | solution.py:626
  62.1 5.3 %collective-permute-start.9 = (f32[64,274]{1,0:T(8,128)S(1)}, f32[64,274]{1,0:T(8,128)S(1)}, u32[]{:S(2)}, u32[]{:S(2)}) collective-permute-start(f32[64,274]{1,0:T(8,128)S(1)} %get-tuple-element.72), channel_id=1, source_target_pairs={{0,15},{1,0},{2,1},{3,2},{4,3},{5,4},{6,5},{7,6},{8,7},{9,8},{10,9... | collective-permute-start | bytes 210440 | tf_op jit(solution)/shard_map/ppermute | solution.py:626
  67.5 2.9 %shard_map.128.field = f32[64,32,274]{2,1,0:T(8,128)S(1)} custom-call(s32[2]{0:T(128)S(1)} %gather_fusion, s32[2,512]{1,0:T(2,128)S(1)} %broadcast_clamp_fusion.cells, bf16[2,512,768]{2,1,0:T(8,128)(2,1)S(1)} %get-tuple-element.68.parts), custom_call_target="tpu_custom_call" | custom-call | flops 4000000000 | bytes 12000000 | tf_op jit(solution)/shard_map/pallas_call | solution.py:470
  70.8 3.2 %collective-permute-start.11 = (f32[1,32,274]{2,1,0:T(8,128)S(1)}, f32[1,32,274]{2,1,0:T(8,128)S(1)}, u32[]{:S(2)}, u32[]{:S(2)}) collective-permute-start(f32[1,32,274]{2,1,0:T(8,128)S(1)} %get-tuple-element.84), channel_id=1, source_target_pairs={{0,48},{16,0},{32,16},{48,32},{1,49},{17,1},{33,17},{49,33},{2,50}... | collective-permute-start | bytes 105224 | tf_op jit(solution)/shard_map/ppermute | solution.py:626
  74.0 5.3 %collective-permute-start.13 = (f32[64,274]{1,0:T(8,128)S(1)}, f32[64,274]{1,0:T(8,128)S(1)}, u32[]{:S(2)}, u32[]{:S(2)}) collective-permute-start(f32[64,274]{1,0:T(8,128)S(1)} %get-tuple-element.86), channel_id=1, source_target_pairs={{0,15},{1,0},{2,1},{3,2},{4,3},{5,4},{6,5},{7,6},{8,7},{9,8},{10,9... | collective-permute-start | bytes 210440 | tf_op jit(solution)/shard_map/ppermute | solution.py:626
  79.4 3.7 %shard_map.129 = (f32[64,32,274]{2,1,0:T(8,128)S(1)}, f32[8,128]{1,0:T(8,128)S(1)}) custom-call(f32[64,32,274]{2,1,0:T(8,128)S(1)} %shard_map.128.field, f32[1,32,274]{2,1,0:T(8,128)S(1)} %collective-permute-done.6.south, f32[1,32,274]{2,1,0:T(8,128)S(1)} %collective-permute-done.7.north, f32[64,274]{1,0:T(8,128)S(1)} %collective-permute-done.8.west, ...), custom_call_target="tpu_custom_call" | custom-call | flops 5000000000 | bytes 15000000 | tf_op jit(solution)/shard_map/pallas_call | solution.py:563
  83.2 4.7 %shard_map.131 = (f32[512,384]{1,0:T(8,128)S(1)}, f32[512,384]{1,0:T(8,128)S(1)}) custom-call(s32[2,512]{1,0:T(2,128)S(1)} %broadcast_clamp_fusion.cells, s32[2]{0:T(128)S(1)} %gather_fusion, f32[64,32,274]{2,1,0:T(8,128)S(1)} %get-tuple-element.74.field.basis, f32[1,32,274]{2,1,0:T(8,128)S(1)} %collective-permute-done.10.south, ...), custom_call_target="tpu_custom_call" | custom-call | flops 6000000000 | bytes 18000000 | tf_op jit(solution)/shard_map/pallas_call | solution.py:218
  90.3 14.0 %shard_map.132 = (bf16[512,768]{1,0:T(8,128)(2,1)S(1)}, bf16[512,768]{1,0:T(8,128)(2,1)S(1)}, f32[8,128]{1,0:T(8,128)S(1)}) custom-call(s32[2]{0:T(128)S(1)} %gather_fusion, f32[512,384]{1,0:T(8,128)S(1)} %get-tuple-element.87.own, f32[512,384]{1,0:T(8,128)S(1)} %collective-permute-done.14.other, bf16[512,1024]{1,0:T(8,128)(2,1)S(1)} %copy-done.9, ...), custom_call_target="tpu_custom_call" | custom-call | flops 12999999488 | bytes 39000000 | tf_op jit(solution)/shard_map/pallas_call | solution.py:335
  104.4 7.5 %shard_map.133 = (bf16[512,1024]{1,0:T(8,128)(2,1)S(1)}, bf16[512,1024]{1,0:T(8,128)(2,1)S(1)}) custom-call(bf16[512,768]{1,0:T(8,128)(2,1)S(1)} %get-tuple-element.90.z_hi, bf16[512,768]{1,0:T(8,128)(2,1)S(1)} %get-tuple-element.91.z_lo, bf16[512,1024]{1,0:T(8,128)(2,1)S(1)} %copy-done.9, bf16[512,1024]{1,0:T(8,128)(2,1)S(1)} %copy-done.11, ...), custom_call_target="tpu_custom_call" | custom-call | flops 8000000000 | bytes 24000000 | tf_op jit(solution)/shard_map/pallas_call | solution.py:355
  111.8 2.6 %shard_map.134 = (f32[512,384]{1,0:T(8,128)S(1)}, f32[512,384]{1,0:T(8,128)S(1)}) custom-call(bf16[512,1024]{1,0:T(8,128)(2,1)S(1)} %get-tuple-element.92.b_hi, bf16[512,1024]{1,0:T(8,128)(2,1)S(1)} %get-tuple-element.93.b_lo, bf16[768,1024]{1,0:T(8,128)(2,1)S(1)} %copy-done.13, bf16[768,1024]{1,0:T(8,128)(2,1)S(1)} %copy-done.15), custom_call_target="tpu_custom_call" | custom-call | flops 3000000000 | bytes 9000000 | tf_op jit(solution)/shard_map/pallas_call | solution.py:368
  123.2 3.5 %collective-permute-start.26 = (f32[8,128]{1,0:T(8,128)S(1)}, f32[8,128]{1,0:T(8,128)S(1)}, u32[]{:S(2)}, u32[]{:S(2)}) collective-permute-start(f32[8,128]{1,0:T(8,128)S(1)} %add_add_fusion.3), channel_id=1, source_target_pairs={{0,3},{1,0},{2,1},{3,2},{4,7},{5,4},{6,5},{7,6},{8,11},{9,8},{10,9... | collective-permute-start | bytes 12296 | tf_op jit(solution)/shard_map/ppermute | solution.py:653
  128.0 3.8 %collective-permute-done.25 = f32[8,128]{1,0:T(8,128)S(1)} collective-permute-done((f32[8,128]{1,0:T(8,128)S(1)}, f32[8,128]{1,0:T(8,128)S(1)}, u32[]{:S(2)}, u32[]{:S(2)}) %collective-permute-start.25) | collective-permute-done | bytes 4128 | tf_op jit(solution)/shard_map/ppermute | solution.py:653
  135.5 2.4 %collective-permute-done.28 = f32[8,128]{1,0:T(8,128)S(1)} collective-permute-done((f32[8,128]{1,0:T(8,128)S(1)}, f32[8,128]{1,0:T(8,128)S(1)}, u32[]{:S(2)}, u32[]{:S(2)}) %collective-permute-start.28) | collective-permute-done | bytes 4128 | tf_op jit(solution)/shard_map/ppermute | solution.py:653
  141.8 3.0 %collective-permute-start.17 = (f32[1,32,274]{2,1,0:T(8,128)S(1)}, f32[1,32,274]{2,1,0:T(8,128)S(1)}, u32[]{:S(2)}, u32[]{:S(2)}) collective-permute-start(f32[1,32,274]{2,1,0:T(8,128)S(1)} %get-tuple-element.98), channel_id=1, source_target_pairs={{0,48},{16,0},{32,16},{48,32},{1,49},{17,1},{33,17},{49,33},{2,50}... | collective-permute-start | bytes 105224 | tf_op jit(solution)/shard_map/ppermute | solution.py:626
  145.7 4.4 %collective-permute-start.19 = (f32[64,274]{1,0:T(8,128)S(1)}, f32[64,274]{1,0:T(8,128)S(1)}, u32[]{:S(2)}, u32[]{:S(2)}) collective-permute-start(f32[64,274]{1,0:T(8,128)S(1)} %get-tuple-element.100), channel_id=1, source_target_pairs={{0,15},{1,0},{2,1},{3,2},{4,3},{5,4},{6,5},{7,6},{8,7},{9,8},{10,9... | collective-permute-start | bytes 210440 | tf_op jit(solution)/shard_map/ppermute | solution.py:626
  150.1 2.9 %shard_map.136.field = f32[64,32,274]{2,1,0:T(8,128)S(1)} custom-call(s32[2]{0:T(128)S(1)} %gather_fusion, s32[2,512]{1,0:T(2,128)S(1)} %broadcast_clamp_fusion.cells, bf16[2,512,768]{2,1,0:T(8,128)(2,1)S(1)} %get-tuple-element.96.parts), custom_call_target="tpu_custom_call" | custom-call | flops 4000000000 | bytes 12000000 | tf_op jit(solution)/shard_map/pallas_call | solution.py:470
  153.1 5.2 %shard_map.137 = (f32[64,32,274]{2,1,0:T(8,128)}, f32[64,32,274]{2,1,0:T(8,128)}) custom-call(f32[64,32,274]{2,1,0:T(8,128)S(1)} %shard_map.136.field, f32[1,32,274]{2,1,0:T(8,128)S(1)} %collective-permute-done.16.south, f32[1,32,274]{2,1,0:T(8,128)S(1)} %collective-permute-done.17.north, f32[64,274]{1,0:T(8,128)S(1)} %collective-permute-done.18.west, ...), custom_call_target="tpu_custom_call" | custom-call | flops 6000000000 | bytes 18000000 | tf_op jit(solution)/shard_map/pallas_call | solution.py:613
  (143 shorter events, 38.8 us)
Async XLA Ops:
  1.5 17.8 %collective-permute-start.1 = (f32[1,32,274]{2,1,0:T(8,128)S(1)}, f32[1,32,274]{2,1,0:T(8,128)S(1)}, u32[]{:S(2)}, u32[]{:S(2)}) collective-permute-start(f32[1,32,274]{2,1,0:T(8,128)S(1)} %get-tuple-element.107), channel_id=1, source_target_pairs={{0,48},{16,0},{32,16},{48,32},{1,49},{17,1},{33,17},{49,33},{2,50}... | collective-permute-start | bytes 105224 | tf_op jit(solution)/shard_map/ppermute | solution.py:626
  4.4 14.9 %collective-permute-start = (f32[1,32,274]{2,1,0:T(8,128)S(1)}, f32[1,32,274]{2,1,0:T(8,128)S(1)}, u32[]{:S(2)}, u32[]{:S(2)}) collective-permute-start(f32[1,32,274]{2,1,0:T(8,128)S(1)} %get-tuple-element.108), channel_id=1, source_target_pairs={{0,16},{16,32},{32,48},{48,0},{1,17},{17,33},{33,49},{49,1},{2,18}... | collective-permute-start | bytes 105224 | tf_op jit(solution)/shard_map/ppermute | solution.py:626
  6.0 13.3 %collective-permute-start.2 = (f32[64,274]{1,0:T(8,128)S(1)}, f32[64,274]{1,0:T(8,128)S(1)}, u32[]{:S(2)}, u32[]{:S(2)}) collective-permute-start(f32[64,274]{1,0:T(8,128)S(1)} %bitcast.53), channel_id=1, source_target_pairs={{0,1},{1,2},{2,3},{3,4},{4,5},{5,6},{6,7},{7,8},{8,9},{9,10},{10,1... | collective-permute-start | bytes 210440 | tf_op jit(solution)/shard_map/ppermute | solution.py:626
  8.0 11.4 %collective-permute-start.3 = (f32[64,274]{1,0:T(8,128)S(1)}, f32[64,274]{1,0:T(8,128)S(1)}, u32[]{:S(2)}, u32[]{:S(2)}) collective-permute-start(f32[64,274]{1,0:T(8,128)S(1)} %bitcast.54), channel_id=1, source_target_pairs={{0,15},{1,0},{2,1},{3,2},{4,3},{5,4},{6,5},{7,6},{8,7},{9,8},{10,9... | collective-permute-start | bytes 210440 | tf_op jit(solution)/shard_map/ppermute | solution.py:626
  58.8 11.6 %collective-permute-start.6 = (f32[1,32,274]{2,1,0:T(8,128)S(1)}, f32[1,32,274]{2,1,0:T(8,128)S(1)}, u32[]{:S(2)}, u32[]{:S(2)}) collective-permute-start(f32[1,32,274]{2,1,0:T(8,128)S(1)} %get-tuple-element.69), channel_id=1, source_target_pairs={{0,16},{16,32},{32,48},{48,0},{1,17},{17,33},{33,49},{49,1},{2,18}... | collective-permute-start | bytes 105224 | tf_op jit(solution)/shard_map/ppermute | solution.py:626
  59.1 11.3 %collective-permute-start.7 = (f32[1,32,274]{2,1,0:T(8,128)S(1)}, f32[1,32,274]{2,1,0:T(8,128)S(1)}, u32[]{:S(2)}, u32[]{:S(2)}) collective-permute-start(f32[1,32,274]{2,1,0:T(8,128)S(1)} %get-tuple-element.70), channel_id=1, source_target_pairs={{0,48},{16,0},{32,16},{48,32},{1,49},{17,1},{33,17},{49,33},{2,50}... | collective-permute-start | bytes 105224 | tf_op jit(solution)/shard_map/ppermute | solution.py:626
  62.1 8.3 %collective-permute-start.8 = (f32[64,274]{1,0:T(8,128)S(1)}, f32[64,274]{1,0:T(8,128)S(1)}, u32[]{:S(2)}, u32[]{:S(2)}) collective-permute-start(f32[64,274]{1,0:T(8,128)S(1)} %get-tuple-element.71), channel_id=1, source_target_pairs={{0,1},{1,2},{2,3},{3,4},{4,5},{5,6},{6,7},{7,8},{8,9},{9,10},{10,1... | collective-permute-start | bytes 210440 | tf_op jit(solution)/shard_map/ppermute | solution.py:626
  62.1 8.3 %collective-permute-start.9 = (f32[64,274]{1,0:T(8,128)S(1)}, f32[64,274]{1,0:T(8,128)S(1)}, u32[]{:S(2)}, u32[]{:S(2)}) collective-permute-start(f32[64,274]{1,0:T(8,128)S(1)} %get-tuple-element.72), channel_id=1, source_target_pairs={{0,15},{1,0},{2,1},{3,2},{4,3},{5,4},{6,5},{7,6},{8,7},{9,8},{10,9... | collective-permute-start | bytes 210440 | tf_op jit(solution)/shard_map/ppermute | solution.py:626
  70.7 12.4 %collective-permute-start.10 = (f32[1,32,274]{2,1,0:T(8,128)S(1)}, f32[1,32,274]{2,1,0:T(8,128)S(1)}, u32[]{:S(2)}, u32[]{:S(2)}) collective-permute-start(f32[1,32,274]{2,1,0:T(8,128)S(1)} %get-tuple-element.83), channel_id=1, source_target_pairs={{0,16},{16,32},{32,48},{48,0},{1,17},{17,33},{33,49},{49,1},{2,18}... | collective-permute-start | bytes 105224 | tf_op jit(solution)/shard_map/ppermute | solution.py:626
  70.8 12.3 %collective-permute-start.11 = (f32[1,32,274]{2,1,0:T(8,128)S(1)}, f32[1,32,274]{2,1,0:T(8,128)S(1)}, u32[]{:S(2)}, u32[]{:S(2)}) collective-permute-start(f32[1,32,274]{2,1,0:T(8,128)S(1)} %get-tuple-element.84), channel_id=1, source_target_pairs={{0,48},{16,0},{32,16},{48,32},{1,49},{17,1},{33,17},{49,33},{2,50}... | collective-permute-start | bytes 105224 | tf_op jit(solution)/shard_map/ppermute | solution.py:626
  74.0 9.1 %collective-permute-start.12 = (f32[64,274]{1,0:T(8,128)S(1)}, f32[64,274]{1,0:T(8,128)S(1)}, u32[]{:S(2)}, u32[]{:S(2)}) collective-permute-start(f32[64,274]{1,0:T(8,128)S(1)} %get-tuple-element.85), channel_id=1, source_target_pairs={{0,1},{1,2},{2,3},{3,4},{4,5},{5,6},{6,7},{7,8},{8,9},{9,10},{10,1... | collective-permute-start | bytes 210440 | tf_op jit(solution)/shard_map/ppermute | solution.py:626
  74.0 9.1 %collective-permute-start.13 = (f32[64,274]{1,0:T(8,128)S(1)}, f32[64,274]{1,0:T(8,128)S(1)}, u32[]{:S(2)}, u32[]{:S(2)}) collective-permute-start(f32[64,274]{1,0:T(8,128)S(1)} %get-tuple-element.86), channel_id=1, source_target_pairs={{0,15},{1,0},{2,1},{3,2},{4,3},{5,4},{6,5},{7,6},{8,7},{9,8},{10,9... | collective-permute-start | bytes 210440 | tf_op jit(solution)/shard_map/ppermute | solution.py:626
  114.5 24.8 %collective-permute-start.15 = (f32[512,384]{1,0:T(8,128)S(1)}, f32[512,384]{1,0:T(8,128)S(1)}, u32[]{:S(2)}, u32[]{:S(2)}) collective-permute-start(f32[512,384]{1,0:T(8,128)S(1)} %get-tuple-element.95), channel_id=1, source_target_pairs={{0,64},{64,0},{1,65},{65,1},{2,66},{66,2},{3,67},{67,3},{4,68},{68... | collective-permute-start | bytes 2359304 | tf_op jit(solution)/shard_map/ppermute | solution.py:638
  116.9 5.1 %collective-permute-start.22 = (f32[8,128]{1,0:T(8,128)S(1)}, f32[8,128]{1,0:T(8,128)S(1)}, u32[]{:S(2)}, u32[]{:S(2)}) collective-permute-start(f32[8,128]{1,0:T(8,128)S(1)} %add.128), channel_id=1, source_target_pairs={{0,32},{16,48},{32,0},{48,16},{1,33},{17,49},{33,1},{49,17},{2,34}... | collective-permute-start | bytes 12296 | tf_op jit(solution)/shard_map/ppermute | solution.py:626
  117.3 5.8 %collective-permute-start.21 = (f32[8,128]{1,0:T(8,128)S(1)}, f32[8,128]{1,0:T(8,128)S(1)}, u32[]{:S(2)}, u32[]{:S(2)}) collective-permute-start(f32[8,128]{1,0:T(8,128)S(1)} %add.128), channel_id=1, source_target_pairs={{0,16},{16,32},{32,48},{48,0},{1,17},{17,33},{33,49},{49,1},{2,18}... | collective-permute-start | bytes 12296 | tf_op jit(solution)/shard_map/ppermute | solution.py:626
  123.2 4.9 %collective-permute-start.26 = (f32[8,128]{1,0:T(8,128)S(1)}, f32[8,128]{1,0:T(8,128)S(1)}, u32[]{:S(2)}, u32[]{:S(2)}) collective-permute-start(f32[8,128]{1,0:T(8,128)S(1)} %add_add_fusion.3), channel_id=1, source_target_pairs={{0,3},{1,0},{2,1},{3,2},{4,7},{5,4},{6,5},{7,6},{8,11},{9,8},{10,9... | collective-permute-start | bytes 12296 | tf_op jit(solution)/shard_map/ppermute | solution.py:653
  126.7 5.1 %collective-permute-start.25 = (f32[8,128]{1,0:T(8,128)S(1)}, f32[8,128]{1,0:T(8,128)S(1)}, u32[]{:S(2)}, u32[]{:S(2)}) collective-permute-start(f32[8,128]{1,0:T(8,128)S(1)} %add_add_fusion.3), channel_id=1, source_target_pairs={{0,2},{1,3},{2,0},{3,1},{4,6},{5,7},{6,4},{7,5},{8,10},{9,11},{10,... | collective-permute-start | bytes 12296 | tf_op jit(solution)/shard_map/ppermute | solution.py:653
  126.7 5.1 %collective-permute-start.24 = (f32[8,128]{1,0:T(8,128)S(1)}, f32[8,128]{1,0:T(8,128)S(1)}, u32[]{:S(2)}, u32[]{:S(2)}) collective-permute-start(f32[8,128]{1,0:T(8,128)S(1)} %add_add_fusion.3), channel_id=1, source_target_pairs={{0,1},{1,2},{2,3},{3,0},{4,5},{5,6},{6,7},{7,4},{8,9},{9,10},{10,1... | collective-permute-start | bytes 12296 | tf_op jit(solution)/shard_map/ppermute | solution.py:653
  132.8 5.1 %collective-permute-start.28 = (f32[8,128]{1,0:T(8,128)S(1)}, f32[8,128]{1,0:T(8,128)S(1)}, u32[]{:S(2)}, u32[]{:S(2)}) collective-permute-start(f32[8,128]{1,0:T(8,128)S(1)} %add_add_fusion.2), channel_id=1, source_target_pairs={{0,8},{1,9},{2,10},{3,11},{4,12},{5,13},{6,14},{7,15},{8,0},{9,1},... | collective-permute-start | bytes 12296 | tf_op jit(solution)/shard_map/ppermute | solution.py:653
  134.5 4.8 %collective-permute-start.27 = (f32[8,128]{1,0:T(8,128)S(1)}, f32[8,128]{1,0:T(8,128)S(1)}, u32[]{:S(2)}, u32[]{:S(2)}) collective-permute-start(f32[8,128]{1,0:T(8,128)S(1)} %add_add_fusion.2), channel_id=1, source_target_pairs={{0,4},{1,5},{2,6},{3,7},{4,8},{5,9},{6,10},{7,11},{8,12},{9,13},{1... | collective-permute-start | bytes 12296 | tf_op jit(solution)/shard_map/ppermute | solution.py:653
  141.6 11.5 %collective-permute-start.16 = (f32[1,32,274]{2,1,0:T(8,128)S(1)}, f32[1,32,274]{2,1,0:T(8,128)S(1)}, u32[]{:S(2)}, u32[]{:S(2)}) collective-permute-start(f32[1,32,274]{2,1,0:T(8,128)S(1)} %get-tuple-element.97), channel_id=1, source_target_pairs={{0,16},{16,32},{32,48},{48,0},{1,17},{17,33},{33,49},{49,1},{2,18}... | collective-permute-start | bytes 105224 | tf_op jit(solution)/shard_map/ppermute | solution.py:626
  141.8 11.3 %collective-permute-start.17 = (f32[1,32,274]{2,1,0:T(8,128)S(1)}, f32[1,32,274]{2,1,0:T(8,128)S(1)}, u32[]{:S(2)}, u32[]{:S(2)}) collective-permute-start(f32[1,32,274]{2,1,0:T(8,128)S(1)} %get-tuple-element.98), channel_id=1, source_target_pairs={{0,48},{16,0},{32,16},{48,32},{1,49},{17,1},{33,17},{49,33},{2,50}... | collective-permute-start | bytes 105224 | tf_op jit(solution)/shard_map/ppermute | solution.py:626
  144.8 8.3 %collective-permute-start.18 = (f32[64,274]{1,0:T(8,128)S(1)}, f32[64,274]{1,0:T(8,128)S(1)}, u32[]{:S(2)}, u32[]{:S(2)}) collective-permute-start(f32[64,274]{1,0:T(8,128)S(1)} %get-tuple-element.99), channel_id=1, source_target_pairs={{0,1},{1,2},{2,3},{3,4},{4,5},{5,6},{6,7},{7,8},{8,9},{9,10},{10,1... | collective-permute-start | bytes 210440 | tf_op jit(solution)/shard_map/ppermute | solution.py:626
  145.7 7.3 %collective-permute-start.19 = (f32[64,274]{1,0:T(8,128)S(1)}, f32[64,274]{1,0:T(8,128)S(1)}, u32[]{:S(2)}, u32[]{:S(2)}) collective-permute-start(f32[64,274]{1,0:T(8,128)S(1)} %get-tuple-element.100), channel_id=1, source_target_pairs={{0,15},{1,0},{2,1},{3,2},{4,3},{5,4},{6,5},{7,6},{8,7},{9,8},{10,9... | collective-permute-start | bytes 210440 | tf_op jit(solution)/shard_map/ppermute | solution.py:626
  (36 other events, 301.6 us)

commit v2 on v1

--- a/solution.py
+++ b/solution.py
@@ -196,13 +196,17 @@
     if with_square:
         rest[0][...] = lane_vector([jnp.sum(total)])
 
+    place = lax.broadcasted_iota(jnp.int32, (8, 128), 0)
+
     def gather(which, out):
         def body(b, carry):
             first = pl.multiple_of(b * 8, 8)
             found = [cells[which, first + k] for k in range(8)]
-            rows = [[image[t, pl.ds(cell, 1), :] for t in range(3)] for cell in found]
-            for k in range(8):
-                out[pl.ds(first + k, 1), :] = jnp.concatenate(rows[k], axis=1)
+            for t in range(3):
+                block = image[t, pl.ds(found[0], 8, stride=0), :]
+                for k in range(1, 8):
+                    block = jnp.where(place == k, image[t, pl.ds(found[k], 8, stride=0), :], block)
+                out[pl.ds(first, 8), t * 128 : (t + 1) * 128] = block
             return carry
 
         lax.fori_loop(0, (counts[which] + 7) // 8, body, 0)
@@ -390,11 +394,13 @@
     lats, lons, _ = coupling.shape
     slots = own.shape[0]
     width = west.shape[1]
-    for k, part in enumerate((own, other)):
-        row = lax.broadcasted_iota(jnp.int32, (slots, WIDE), 0)
-        upper, lower = halves_of(jnp.where(row < counts[k], part[...], 0.0))
-        parts[k, :, 0:WIDE] = upper
-        parts[k, :, WIDE : 2 * WIDE] = lower
+    pieces = [(k, s) for s in range(0, slots, BLOCK) for k in range(2)]
+    for b, (k, s) in enumerate(pieces):
+        row = lax.broadcasted_iota(jnp.int32, (BLOCK, WIDE), 0) + s
+        part = (own, other)[k][s : s + BLOCK, :]
+        upper, lower = halves_of(jnp.where(row < counts[k], part, 0.0))
+        parts[b, :, 0:WIDE] = upper
+        parts[b, :, WIDE : 2 * WIDE] = lower
     total = 4 * lats + 4 * lons
     r = lax.broadcasted_iota(jnp.int32, (total, BLOCK), 0)
     cell = jnp.full_like(r, -1)
@@ -411,10 +417,9 @@
         spans.append((start, lons))
         start += lons
     value = jnp.zeros((total, 2 * WIDE), f32)
-    for k in range(2):
-        for s in range(0, slots, BLOCK):
-            hot = hot_rows(cell, cells[k : k + 1, s : s + BLOCK])
-            value = value + jnp.dot(hot, parts[k, s : s + BLOCK, :], preferred_element_type=f32)
+    for b in range(len(pieces)):
+        hot = hot_rows(cell, cells[b : b + 1, :])
+        value = value + jnp.dot(hot, parts[b], preferred_element_type=f32)
     value = merged(value)[:, :width]
     for line, (start, count) in zip(lines, spans):
         line[...] = value[start : start + count]
@@ -431,7 +436,7 @@
 def edge_call(counts, cells, own, other, coupling, columns, width):
     lats, lons, _ = coupling.shape
     slots = own.shape[0]
-    out = [shape((2, slots, 2 * WIDE), bf16)] + edge_shapes(lats, lons, width)
+    out = [shape((2 * slots // BLOCK, BLOCK, 2 * WIDE), bf16)] + edge_shapes(lats, lons, width)
     out += [shape((lats, width))] * 4 + [shape((lons, width))] * 4
     return call(edge_kernel, out, [smem] + [vmem] * 5, [vmem] * len(out), [], 12, 2)(
         counts, cells, own, other, coupling, columns
@@ -440,26 +445,34 @@
 
 def spread_kernel(counts, cells, parts, field):
     lats, lons, width = field.shape
-    slots = parts.shape[1]
-    chunk = 512
+    chunk = 256
+    upper = [counts[k] > BLOCK for k in range(2)]
 
     def body(b, carry):
-        first = b * chunk
-        cell = lax.broadcasted_iota(jnp.int32, (chunk, BLOCK), 0) + first
+        cell = lax.broadcasted_iota(jnp.int32, (chunk, BLOCK), 0) + b * chunk
         lat = pl.ds(b * (chunk // lons), chunk // lons)
 
-        def piece(k, s):
-            hot = hot_rows(cell, cells[k : k + 1, s : s + BLOCK])
-            both = jnp.dot(hot, parts[k, s : s + BLOCK, :], preferred_element_type=f32)
-            return merged(both)[:, :width].reshape(chunk // lons, lons, width)
-
-        field[lat] = piece(0, 0) + piece(1, 0)
-        for k in range(2):
-            for s in range(BLOCK, slots, BLOCK):
-
-                @pl.when(counts[k] > s)
-                def _(k=k, s=s):
-                    field[lat] += piece(k, s)
+        def product(blocks):
+            hot = [hot_rows(cell, cells[pl.ds(k, 1), :]) for k in blocks]
+            part = [parts[k] for k in blocks]
+            both = jnp.dot(
+                jnp.concatenate(hot, axis=1),
+                jnp.concatenate(part, axis=0),
+                preferred_element_type=f32,
+            )
+            field[lat] = merged(both)[:, :width].reshape(chunk // lons, lons, width)
+
+        @pl.when(upper[0] & upper[1])
+        def _():
+            product((0, 1, 2, 3))
+
+        @pl.when(upper[0] != upper[1])
+        def _():
+            product((0, 1, jnp.where(upper[0], 2, 3)))
+
+        @pl.when(jnp.logical_not(upper[0] | upper[1]))
+        def _():
+            product((0, 1))
 
         return carry
 
@@ -674,23 +687,21 @@
     halo = exchanged(
         right_side[:1], right_side[lats - 1 :], right_side[:, 0], right_side[:, lons - 1]
     )
-    latitude = lax.axis_index("row") * lats + jnp.arange(lats)
-    north_open = (latitude < lats * lax.axis_size("row") - 1)[:, None]
-    south_open = (latitude > 0)[:, None]
-    planes = [
-        couplings[0],
-        couplings[1],
-        jnp.where(north_open, couplings[2], 0.0),
-        jnp.where(south_open, couplings[3], 0.0),
-    ]
-    planes.append(planes[0] + planes[1] + planes[2] + planes[3])
-    coupling = jnp.stack(planes, axis=2)
+    latitude = lax.axis_index("row") * lats + jnp.arange(lats)[None, :, None]
+    plane = jnp.arange(4)[:, None, None]
+    closed = (plane == 2) & (latitude == lats * lax.axis_size("row") - 1)
+    closed = closed | ((plane == 3) & (latitude == 0))
+    planes = jnp.where(closed, 0.0, couplings)
+    planes = jnp.concatenate([planes, jnp.sum(planes, axis=0, keepdims=True)], axis=0)
+    coupling = jnp.transpose(planes, (1, 2, 0))
     pick = ((0, lons - 1), (1, 0), (1, 1), (2, 0), (3, 0), (4, 0))
     pick += ((0, lons - 2), (2, lons - 1), (3, lons - 1), (4, lons - 1))
     columns = jnp.stack([planes[k][:, j] for k, j in pick], axis=1)
     rates = channel_rates[None, :]
     order = jnp.stack([side_index, 1 - side_index])
-    cells = jnp.clip(profile_cells[order], 0, lats * lons - 1)
+    cells = jnp.where(side_index == 0, profile_cells, profile_cells[::-1])
+    cells = jnp.clip(cells, 0, lats * lons - 1)
+    pieces = cells.reshape(2, -1, BLOCK).transpose(1, 0, 2).reshape(-1, BLOCK)
     counts = profile_counts[order * tile_count + tile_index]
     weights = prepare_call(
         order[:1], weight_in, weight_mid, weight_out.T, inverse_cov, 3 * BLOCK
@@ -702,9 +713,9 @@
     back = backward_call(z, gates, weights)
     own, other = gradient_call(1.0 / SCALE, back, weights)
     other = swapped(other)
-    parts, *out = edge_call(counts, cells, own, other, coupling, columns, width)
+    parts, *out = edge_call(counts, pieces, own, other, coupling, columns, width)
     halo = exchanged(*out[:4])
-    field = spread_call(counts, cells, parts, lats, lons, width)
+    field = spread_call(counts, pieces, parts, lats, lons, width)
     outer = border_call(halo, out[4:], coupling, columns, rates)
     outer = exchanged(*outer)
     basis, sums = basis_call(field, halo, coupling, rates, right_side, sums)
@@ -714,9 +725,9 @@
     back = backward_call(z, gates, weights)
     own, other = gradient_call(1.0, back, weights)
     other = swapped(other)
-    parts, *out = edge_call(counts, cells, own, other, coupling, columns, width)
+    parts, *out = edge_call(counts, pieces, own, other, coupling, columns, width)
     halo = exchanged(*out[:4])
-    field = spread_call(counts, cells, parts, lats, lons, width)
+    field = spread_call(counts, pieces, parts, lats, lons, width)
     return tuple(final_call(field, halo, coupling, rates, right_side, basis, sums))
 
 

time: 159 us -> 171 us (1.075)
  local copies, waits for them, and re-layouts: 8.87 us -> 19.2 us
  Pallas kernels: 80.5 us -> 84 us
    unnamed x64 -> x76, local copies, waits for them, and re-layouts: 3.49 us -> 12.2 us
    pallas_call x2, Pallas kernels: 5.78 us -> 7.5 us  [spread_call(): call(spread_kernel, [shape((lats, lons, width))], [smem] + [vmem] * 2, [v...]
  transfers between devices with their start and end apart: 30 -> 30, of which waited for: 11 -> 10; matrix products, arithmetic and copies ran while one was open for 5% -> 5% of each run, Pallas kernels for 9% -> 9%
where the time goes in v2:
time: 171 us; the launch traced here: 170 us
  Pallas kernels  84 us (49%)
  starting transfers between devices  45.4 us (27%)
  local copies, waits for them, and re-layouts  19.2 us (11%)
  waiting for transfers between devices  18.4 us (11%)
  other arithmetic  1.76 us (1%)
    ppermute x19, starting transfers between devices, shifted(): lax.ppermute(value, axis, [(i, (i + step) % count) for i in range(count)])  37.5 us
    pallas_call x2, Pallas kernels, forward_call(): call(functools.partial(forward_kernel, with_sums), out, [smem] + [vmem] *...  28.9 us
    pallas_call x2, Pallas kernels, backward_call(): call(backward_kernel, [shape((rows, hidden), bf16)] * 2, [vmem] * len(arg...  15 us
    unnamed x76, local copies, waits for them, and re-layouts  12.2 us
    pallas_call x2, Pallas kernels, tangent_call(): call(functools.partial(tangent_kernel, with_square), out, [smem, smem] +...  10 us
    ppermute x6, waiting for transfers between devices, everyone(): total = total + lax.ppermute(base, 'col', pairs)  8.33 us
    pallas_call x2, Pallas kernels, spread_call(): call(spread_kernel, [shape((lats, lons, width))], [smem] + [vmem] * 2, [v...  7.5 us
    ppermute x6, starting transfers between devices, everyone(): total = total + lax.ppermute(base, 'col', pairs)  6.45 us
  transfers between devices with their start and end apart: 30, of which 10 were waited for; matrix products, arithmetic and copies ran while one was open for 5% of the time, Pallas kernels for 9%

profile of v2, /device:TPU:0, one launch (start us, length us, event | category | flops | bytes accessed | tf_op | source)
XLA Modules:
  0.0 170.3 jit_solution(9374565923289460858)
XLA Ops:
  1.5 2.9 %collective-permute-start.1 = (f32[1,32,274]{2,1,0:T(8,128)S(1)}, f32[1,32,274]{2,1,0:T(8,128)S(1)}, u32[]{:S(2)}, u32[]{:S(2)}) collective-permute-start(f32[1,32,274]{2,1,0:T(8,128)S(1)} %get-tuple-element.106), channel_id=1, source_target_pairs={{0,48},{16,0},{32,16},{48,32},{1,49},{17,1},{33,17},{49,33},{2,50}... | collective-permute-start | bytes 105224 | tf_op jit(solution)/shard_map/ppermute | solution.py:639
  7.9 4.7 %collective-permute-start.3 = (f32[64,274]{1,0:T(8,128)S(1)}, f32[64,274]{1,0:T(8,128)S(1)}, u32[]{:S(2)}, u32[]{:S(2)}) collective-permute-start(f32[64,274]{1,0:T(8,128)S(1)} %bitcast.35), channel_id=1, source_target_pairs={{0,15},{1,0},{2,1},{3,2},{4,3},{5,4},{6,5},{7,6},{8,7},{9,8},{10,9... | collective-permute-start | bytes 210440 | tf_op jit(solution)/shard_map/ppermute | solution.py:639
  23.4 5.5 %shard_map.122 = (f32[512,384]{1,0:T(8,128)S(1)}, f32[512,384]{1,0:T(8,128)}, f32[8,128]{1,0:T(8,128)S(1)}) custom-call(s32[2,512]{1,0:T(2,128)S(1)} %select_clamp_fusion.cells, s32[2]{0:T(128)S(1)} %gather_fusion, f32[64,32,274]{2,1,0:T(8,128)S(1)} %copy-done.2, f32[1,32,274]{2,1,0:T(8,128)S(1)} %copy-done.15, f32[1,32,274]{2,1,0:T(8,128)S(1)} %copy-done.13, ...), custom_call_target="tpu_custom_call" | custom-call | flops 6000000000 | bytes 18000000 | tf_op jit(solution)/shard_map/pallas_call | solution.py:222
  36.5 4.4 %shard_map.123 = (bf16[768,1024]{1,0:T(8,128)(2,1)S(1)}, bf16[768,1024]{1,0:T(8,128)(2,1)S(1)}, bf16[1024,1024]{1,0:T(8,128)(2,1)S(1)}, bf16[1024,1024]{1,0:T(8,...) custom-call(s32[1]{0:T(128)} %bitcast.9.side, ...), custom_call_target="tpu_custom_call" | custom-call | flops 5000000000 | bytes 15000000 | tf_op jit(solution)/shard_map/pallas_call | solution.py:152
  41.0 14.9 %shard_map.124 = (bf16[512,768]{1,0:T(8,128)(2,1)S(1)}, bf16[512,768]{1,0:T(8,128)(2,1)S(1)}) custom-call(s32[2]{0:T(128)S(1)} %gather_fusion, f32[512,384]{1,0:T(8,128)S(1)} %copy-done.33, f32[512,384]{1,0:T(8,128)} %collective-permute-done.4.other, bf16[512,1024]{1,0:T(8,128)(2,1)S(1)} %copy-done.8, bf16[512,1024]{1,0:T(8,128)(2,1)S(1)} %copy-done.10, ...), custom_call_target="tpu_custom_call" | custom-call | flops 12999999488 | bytes 39000000 | tf_op jit(solution)/shard_map/pallas_call | solution.py:339
  55.9 7.5 %shard_map.125 = (bf16[512,1024]{1,0:T(8,128)(2,1)S(1)}, bf16[512,1024]{1,0:T(8,128)(2,1)S(1)}) custom-call(bf16[512,768]{1,0:T(8,128)(2,1)S(1)} %get-tuple-element.62.z_hi, bf16[512,768]{1,0:T(8,128)(2,1)S(1)} %get-tuple-element.63.z_lo, bf16[512,1024]{1,0:T(8,128)(2,1)S(1)} %copy-done.8, bf16[512,1024]{1,0:T(8,128)(2,1)S(1)} %copy-done.10, ...), custom_call_target="tpu_custom_call" | custom-call | flops 8000000000 | bytes 24000000 | tf_op jit(solution)/shard_map/pallas_call | solution.py:359
  63.5 2.6 %shard_map.126 = (f32[512,384]{1,0:T(8,128)S(1)}, f32[512,384]{1,0:T(8,128)S(1)}) custom-call(bf16[512,1024]{1,0:T(8,128)(2,1)S(1)} %get-tuple-element.64.b_hi, bf16[512,1024]{1,0:T(8,128)(2,1)S(1)} %get-tuple-element.65.b_lo, bf16[768,1024]{1,0:T(8,128)(2,1)S(1)} %get-tuple-element.54.in_hi, bf16[768,1024]{1,0:T(8,128)(2,1)S(1)} %get-tuple-element.55.in_lo), custom_call_target="tpu_custom_call" | custom-call | flops 3000000000 | bytes 9000000 | tf_op jit(solution)/shard_map/pallas_call | solution.py:372
  70.7 2.9 %collective-permute-start.7 = (f32[1,32,274]{2,1,0:T(8,128)S(1)}, f32[1,32,274]{2,1,0:T(8,128)S(1)}, u32[]{:S(2)}, u32[]{:S(2)}) collective-permute-start(f32[1,32,274]{2,1,0:T(8,128)S(1)} %get-tuple-element.70), channel_id=1, source_target_pairs={{0,48},{16,0},{32,16},{48,32},{1,49},{17,1},{33,17},{49,33},{2,50}... | collective-permute-start | bytes 105224 | tf_op jit(solution)/shard_map/ppermute | solution.py:639
  73.6 5.3 %collective-permute-start.9 = (f32[64,274]{1,0:T(8,128)S(1)}, f32[64,274]{1,0:T(8,128)S(1)}, u32[]{:S(2)}, u32[]{:S(2)}) collective-permute-start(f32[64,274]{1,0:T(8,128)S(1)} %get-tuple-element.72), channel_id=1, source_target_pairs={{0,15},{1,0},{2,1},{3,2},{4,3},{5,4},{6,5},{7,6},{8,7},{9,8},{10,9... | collective-permute-start | bytes 210440 | tf_op jit(solution)/shard_map/ppermute | solution.py:639
  79.0 3.7 %shard_map.128.field = f32[64,32,274]{2,1,0:T(8,128)S(1)} custom-call(s32[2]{0:T(128)S(1)} %gather_fusion, s32[4,256]{1,0:T(4,128)S(1)} %reshape.140.cells, bf16[4,256,768]{2,1,0:T(8,128)(2,1)S(1)} %get-tuple-element.68.parts), custom_call_target="tpu_custom_call" | custom-call | flops 4000000000 | bytes 12000000 | tf_op jit(solution)/shard_map/pallas_call | solution.py:483
  83.2 3.2 %collective-permute-start.11 = (f32[1,32,274]{2,1,0:T(8,128)S(1)}, f32[1,32,274]{2,1,0:T(8,128)S(1)}, u32[]{:S(2)}, u32[]{:S(2)}) collective-permute-start(f32[1,32,274]{2,1,0:T(8,128)S(1)} %get-tuple-element.84), channel_id=1, source_target_pairs={{0,48},{16,0},{32,16},{48,32},{1,49},{17,1},{33,17},{49,33},{2,50}... | collective-permute-start | bytes 105224 | tf_op jit(solution)/shard_map/ppermute | solution.py:639
  86.4 5.3 %collective-permute-start.13 = (f32[64,274]{1,0:T(8,128)S(1)}, f32[64,274]{1,0:T(8,128)S(1)}, u32[]{:S(2)}, u32[]{:S(2)}) collective-permute-start(f32[64,274]{1,0:T(8,128)S(1)} %get-tuple-element.86), channel_id=1, source_target_pairs={{0,15},{1,0},{2,1},{3,2},{4,3},{5,4},{6,5},{7,6},{8,7},{9,8},{10,9... | collective-permute-start | bytes 210440 | tf_op jit(solution)/shard_map/ppermute | solution.py:639
  91.7 3.7 %shard_map.129 = (f32[64,32,274]{2,1,0:T(8,128)S(1)}, f32[8,128]{1,0:T(8,128)S(1)}) custom-call(f32[64,32,274]{2,1,0:T(8,128)S(1)} %shard_map.128.field, f32[1,32,274]{2,1,0:T(8,128)S(1)} %collective-permute-done.6.south, f32[1,32,274]{2,1,0:T(8,128)S(1)} %collective-permute-done.7.north, f32[64,274]{1,0:T(8,128)S(1)} %collective-permute-done.8.west, ...), custom_call_target="tpu_custom_call" | custom-call | flops 5000000000 | bytes 15000000 | tf_op jit(solution)/shard_map/pallas_call | solution.py:576
  95.6 4.5 %shard_map.131 = (f32[512,384]{1,0:T(8,128)S(1)}, f32[512,384]{1,0:T(8,128)S(1)}) custom-call(s32[2,512]{1,0:T(2,128)S(1)} %select_clamp_fusion.cells, s32[2]{0:T(128)S(1)} %gather_fusion, f32[64,32,274]{2,1,0:T(8,128)S(1)} %get-tuple-element.74.field.basis, f32[1,32,274]{2,1,0:T(8,128)S(1)} %collective-permute-done.10.south, ...), custom_call_target="tpu_custom_call" | custom-call | flops 6000000000 | bytes 18000000 | tf_op jit(solution)/shard_map/pallas_call | solution.py:222
  102.6 14.0 %shard_map.132 = (bf16[512,768]{1,0:T(8,128)(2,1)S(1)}, bf16[512,768]{1,0:T(8,128)(2,1)S(1)}, f32[8,128]{1,0:T(8,128)S(1)}) custom-call(s32[2]{0:T(128)S(1)} %gather_fusion, f32[512,384]{1,0:T(8,128)S(1)} %get-tuple-element.87.own, f32[512,384]{1,0:T(8,128)S(1)} %collective-permute-done.14.other, bf16[512,1024]{1,0:T(8,128)(2,1)S(1)} %copy-done.9, ...), custom_call_target="tpu_custom_call" | custom-call | flops 12999999488 | bytes 39000000 | tf_op jit(solution)/shard_map/pallas_call | solution.py:339
  116.6 7.5 %shard_map.133 = (bf16[512,1024]{1,0:T(8,128)(2,1)S(1)}, bf16[512,1024]{1,0:T(8,128)(2,1)S(1)}) custom-call(bf16[512,768]{1,0:T(8,128)(2,1)S(1)} %get-tuple-element.90.z_hi, bf16[512,768]{1,0:T(8,128)(2,1)S(1)} %get-tuple-element.91.z_lo, bf16[512,1024]{1,0:T(8,128)(2,1)S(1)} %copy-done.9, bf16[512,1024]{1,0:T(8,128)(2,1)S(1)} %copy-done.11, ...), custom_call_target="tpu_custom_call" | custom-call | flops 8000000000 | bytes 24000000 | tf_op jit(solution)/shard_map/pallas_call | solution.py:359
  124.1 2.6 %shard_map.134 = (f32[512,384]{1,0:T(8,128)S(1)}, f32[512,384]{1,0:T(8,128)S(1)}) custom-call(bf16[512,1024]{1,0:T(8,128)(2,1)S(1)} %get-tuple-element.92.b_hi, bf16[512,1024]{1,0:T(8,128)(2,1)S(1)} %get-tuple-element.93.b_lo, bf16[768,1024]{1,0:T(8,128)(2,1)S(1)} %copy-done.17, bf16[768,1024]{1,0:T(8,128)(2,1)S(1)} %copy-done.19), custom_call_target="tpu_custom_call" | custom-call | flops 3000000000 | bytes 9000000 | tf_op jit(solution)/shard_map/pallas_call | solution.py:372
  139.0 3.1 %collective-permute-done.25 = f32[8,128]{1,0:T(8,128)S(1)} collective-permute-done((f32[8,128]{1,0:T(8,128)S(1)}, f32[8,128]{1,0:T(8,128)S(1)}, u32[]{:S(2)}, u32[]{:S(2)}) %collective-permute-start.25) | collective-permute-done | bytes 4128 | tf_op jit(solution)/shard_map/ppermute | solution.py:666
  142.1 3.0 %collective-permute-start.29 = (f32[8,128]{1,0:T(8,128)S(1)}, f32[8,128]{1,0:T(8,128)S(1)}, u32[]{:S(2)}, u32[]{:S(2)}) collective-permute-start(f32[8,128]{1,0:T(8,128)S(1)} %add_add_fusion.1), channel_id=1, source_target_pairs={{0,12},{1,13},{2,14},{3,15},{4,0},{5,1},{6,2},{7,3},{8,4},{9,5},{1... | collective-permute-start | bytes 12296 | tf_op jit(solution)/shard_map/ppermute | solution.py:666
  146.4 3.8 %collective-permute-done.28 = f32[8,128]{1,0:T(8,128)S(1)} collective-permute-done((f32[8,128]{1,0:T(8,128)S(1)}, f32[8,128]{1,0:T(8,128)S(1)}, u32[]{:S(2)}, u32[]{:S(2)}) %collective-permute-start.28) | collective-permute-done | bytes 4128 | tf_op jit(solution)/shard_map/ppermute | solution.py:666
  153.4 2.3 %collective-permute-start.17 = (f32[1,32,274]{2,1,0:T(8,128)S(1)}, f32[1,32,274]{2,1,0:T(8,128)S(1)}, u32[]{:S(2)}, u32[]{:S(2)}) collective-permute-start(f32[1,32,274]{2,1,0:T(8,128)S(1)} %get-tuple-element.98), channel_id=1, source_target_pairs={{0,48},{16,0},{32,16},{48,32},{1,49},{17,1},{33,17},{49,33},{2,50}... | collective-permute-start | bytes 105224 | tf_op jit(solution)/shard_map/ppermute | solution.py:639
  155.9 5.2 %collective-permute-start.19 = (f32[64,274]{1,0:T(8,128)S(1)}, f32[64,274]{1,0:T(8,128)S(1)}, u32[]{:S(2)}, u32[]{:S(2)}) collective-permute-start(f32[64,274]{1,0:T(8,128)S(1)} %get-tuple-element.100), channel_id=1, source_target_pairs={{0,15},{1,0},{2,1},{3,2},{4,3},{5,4},{6,5},{7,6},{8,7},{9,8},{10,9... | collective-permute-start | bytes 210440 | tf_op jit(solution)/shard_map/ppermute | solution.py:639
  161.1 3.8 %shard_map.136.field = f32[64,32,274]{2,1,0:T(8,128)S(1)} custom-call(s32[2]{0:T(128)S(1)} %gather_fusion, s32[4,256]{1,0:T(4,128)S(1)} %reshape.140.cells, bf16[4,256,768]{2,1,0:T(8,128)(2,1)S(1)} %get-tuple-element.96.parts), custom_call_target="tpu_custom_call" | custom-call | flops 4000000000 | bytes 12000000 | tf_op jit(solution)/shard_map/pallas_call | solution.py:483
  164.9 5.2 %shard_map.137 = (f32[64,32,274]{2,1,0:T(8,128)}, f32[64,32,274]{2,1,0:T(8,128)}) custom-call(f32[64,32,274]{2,1,0:T(8,128)S(1)} %shard_map.136.field, f32[1,32,274]{2,1,0:T(8,128)S(1)} %collective-permute-done.16.south, f32[1,32,274]{2,1,0:T(8,128)S(1)} %collective-permute-done.17.north, f32[64,274]{1,0:T(8,128)S(1)} %collective-permute-done.18.west, ...), custom_call_target="tpu_custom_call" | custom-call | flops 6000000000 | bytes 18000000 | tf_op jit(solution)/shard_map/pallas_call | solution.py:626
  (155 shorter events, 47.1 us)
Async XLA Ops:
  1.5 17.2 %collective-permute-start.1 = (f32[1,32,274]{2,1,0:T(8,128)S(1)}, f32[1,32,274]{2,1,0:T(8,128)S(1)}, u32[]{:S(2)}, u32[]{:S(2)}) collective-permute-start(f32[1,32,274]{2,1,0:T(8,128)S(1)} %get-tuple-element.106), channel_id=1, source_target_pairs={{0,48},{16,0},{32,16},{48,32},{1,49},{17,1},{33,17},{49,33},{2,50}... | collective-permute-start | bytes 105224 | tf_op jit(solution)/shard_map/ppermute | solution.py:639
  4.4 14.8 %collective-permute-start = (f32[1,32,274]{2,1,0:T(8,128)S(1)}, f32[1,32,274]{2,1,0:T(8,128)S(1)}, u32[]{:S(2)}, u32[]{:S(2)}) collective-permute-start(f32[1,32,274]{2,1,0:T(8,128)S(1)} %get-tuple-element.107), channel_id=1, source_target_pairs={{0,16},{16,32},{32,48},{48,0},{1,17},{17,33},{33,49},{49,1},{2,18}... | collective-permute-start | bytes 105224 | tf_op jit(solution)/shard_map/ppermute | solution.py:639
  5.9 13.9 %collective-permute-start.2 = (f32[64,274]{1,0:T(8,128)S(1)}, f32[64,274]{1,0:T(8,128)S(1)}, u32[]{:S(2)}, u32[]{:S(2)}) collective-permute-start(f32[64,274]{1,0:T(8,128)S(1)} %bitcast.34), channel_id=1, source_target_pairs={{0,1},{1,2},{2,3},{3,4},{4,5},{5,6},{6,7},{7,8},{8,9},{9,10},{10,1... | collective-permute-start | bytes 210440 | tf_op jit(solution)/shard_map/ppermute | solution.py:639
  7.9 11.9 %collective-permute-start.3 = (f32[64,274]{1,0:T(8,128)S(1)}, f32[64,274]{1,0:T(8,128)S(1)}, u32[]{:S(2)}, u32[]{:S(2)}) collective-permute-start(f32[64,274]{1,0:T(8,128)S(1)} %bitcast.35), channel_id=1, source_target_pairs={{0,15},{1,0},{2,1},{3,2},{4,3},{5,4},{6,5},{7,6},{8,7},{9,8},{10,9... | collective-permute-start | bytes 210440 | tf_op jit(solution)/shard_map/ppermute | solution.py:639
  30.4 10.6 %collective-permute-start.4 = (f32[512,384]{1,0:T(8,128)}, f32[512,384]{1,0:T(8,128)}, u32[]{:S(2)}, u32[]{:S(2)}) collective-permute-start(f32[512,384]{1,0:T(8,128)} %get-tuple-element.53), channel_id=1, source_target_pairs={{0,64},{64,0},{1,65},{65,1},{2,66},{66,2},{3,67},{67,3},{4,68},{68... | collective-permute-start | bytes 2359304 | tf_op jit(solution)/shard_map/ppermute | solution.py:651
  70.3 12.4 %collective-permute-start.6 = (f32[1,32,274]{2,1,0:T(8,128)S(1)}, f32[1,32,274]{2,1,0:T(8,128)S(1)}, u32[]{:S(2)}, u32[]{:S(2)}) collective-permute-start(f32[1,32,274]{2,1,0:T(8,128)S(1)} %get-tuple-element.69), channel_id=1, source_target_pairs={{0,16},{16,32},{32,48},{48,0},{1,17},{17,33},{33,49},{49,1},{2,18}... | collective-permute-start | bytes 105224 | tf_op jit(solution)/shard_map/ppermute | solution.py:639
  70.7 12.0 %collective-permute-start.7 = (f32[1,32,274]{2,1,0:T(8,128)S(1)}, f32[1,32,274]{2,1,0:T(8,128)S(1)}, u32[]{:S(2)}, u32[]{:S(2)}) collective-permute-start(f32[1,32,274]{2,1,0:T(8,128)S(1)} %get-tuple-element.70), channel_id=1, source_target_pairs={{0,48},{16,0},{32,16},{48,32},{1,49},{17,1},{33,17},{49,33},{2,50}... | collective-permute-start | bytes 105224 | tf_op jit(solution)/shard_map/ppermute | solution.py:639
  73.6 9.1 %collective-permute-start.8 = (f32[64,274]{1,0:T(8,128)S(1)}, f32[64,274]{1,0:T(8,128)S(1)}, u32[]{:S(2)}, u32[]{:S(2)}) collective-permute-start(f32[64,274]{1,0:T(8,128)S(1)} %get-tuple-element.71), channel_id=1, source_target_pairs={{0,1},{1,2},{2,3},{3,4},{4,5},{5,6},{6,7},{7,8},{8,9},{9,10},{10,1... | collective-permute-start | bytes 210440 | tf_op jit(solution)/shard_map/ppermute | solution.py:639
  73.6 9.2 %collective-permute-start.9 = (f32[64,274]{1,0:T(8,128)S(1)}, f32[64,274]{1,0:T(8,128)S(1)}, u32[]{:S(2)}, u32[]{:S(2)}) collective-permute-start(f32[64,274]{1,0:T(8,128)S(1)} %get-tuple-element.72), channel_id=1, source_target_pairs={{0,15},{1,0},{2,1},{3,2},{4,3},{5,4},{6,5},{7,6},{8,7},{9,8},{10,9... | collective-permute-start | bytes 210440 | tf_op jit(solution)/shard_map/ppermute | solution.py:639
  83.1 12.4 %collective-permute-start.10 = (f32[1,32,274]{2,1,0:T(8,128)S(1)}, f32[1,32,274]{2,1,0:T(8,128)S(1)}, u32[]{:S(2)}, u32[]{:S(2)}) collective-permute-start(f32[1,32,274]{2,1,0:T(8,128)S(1)} %get-tuple-element.83), channel_id=1, source_target_pairs={{0,16},{16,32},{32,48},{48,0},{1,17},{17,33},{33,49},{49,1},{2,18}... | collective-permute-start | bytes 105224 | tf_op jit(solution)/shard_map/ppermute | solution.py:639
  83.2 12.3 %collective-permute-start.11 = (f32[1,32,274]{2,1,0:T(8,128)S(1)}, f32[1,32,274]{2,1,0:T(8,128)S(1)}, u32[]{:S(2)}, u32[]{:S(2)}) collective-permute-start(f32[1,32,274]{2,1,0:T(8,128)S(1)} %get-tuple-element.84), channel_id=1, source_target_pairs={{0,48},{16,0},{32,16},{48,32},{1,49},{17,1},{33,17},{49,33},{2,50}... | collective-permute-start | bytes 105224 | tf_op jit(solution)/shard_map/ppermute | solution.py:639
  86.4 9.1 %collective-permute-start.12 = (f32[64,274]{1,0:T(8,128)S(1)}, f32[64,274]{1,0:T(8,128)S(1)}, u32[]{:S(2)}, u32[]{:S(2)}) collective-permute-start(f32[64,274]{1,0:T(8,128)S(1)} %get-tuple-element.85), channel_id=1, source_target_pairs={{0,1},{1,2},{2,3},{3,4},{4,5},{5,6},{6,7},{7,8},{8,9},{9,10},{10,1... | collective-permute-start | bytes 210440 | tf_op jit(solution)/shard_map/ppermute | solution.py:639
  86.4 9.1 %collective-permute-start.13 = (f32[64,274]{1,0:T(8,128)S(1)}, f32[64,274]{1,0:T(8,128)S(1)}, u32[]{:S(2)}, u32[]{:S(2)}) collective-permute-start(f32[64,274]{1,0:T(8,128)S(1)} %get-tuple-element.86), channel_id=1, source_target_pairs={{0,15},{1,0},{2,1},{3,2},{4,3},{5,4},{6,5},{7,6},{8,7},{9,8},{10,9... | collective-permute-start | bytes 210440 | tf_op jit(solution)/shard_map/ppermute | solution.py:639
  126.7 23.5 %collective-permute-start.15 = (f32[512,384]{1,0:T(8,128)S(1)}, f32[512,384]{1,0:T(8,128)S(1)}, u32[]{:S(2)}, u32[]{:S(2)}) collective-permute-start(f32[512,384]{1,0:T(8,128)S(1)} %get-tuple-element.95), channel_id=1, source_target_pairs={{0,64},{64,0},{1,65},{65,1},{2,66},{66,2},{3,67},{67,3},{4,68},{68... | collective-permute-start | bytes 2359304 | tf_op jit(solution)/shard_map/ppermute | solution.py:651
  129.1 5.1 %collective-permute-start.22 = (f32[8,128]{1,0:T(8,128)S(1)}, f32[8,128]{1,0:T(8,128)S(1)}, u32[]{:S(2)}, u32[]{:S(2)}) collective-permute-start(f32[8,128]{1,0:T(8,128)S(1)} %add.76), channel_id=1, source_target_pairs={{0,32},{16,48},{32,0},{48,16},{1,33},{17,49},{33,1},{49,17},{2,34}... | collective-permute-start | bytes 12296 | tf_op jit(solution)/shard_map/ppermute | solution.py:639
  129.6 5.8 %collective-permute-start.21 = (f32[8,128]{1,0:T(8,128)S(1)}, f32[8,128]{1,0:T(8,128)S(1)}, u32[]{:S(2)}, u32[]{:S(2)}) collective-permute-start(f32[8,128]{1,0:T(8,128)S(1)} %add.76), channel_id=1, source_target_pairs={{0,16},{16,32},{32,48},{48,0},{1,17},{17,33},{33,49},{49,1},{2,18}... | collective-permute-start | bytes 12296 | tf_op jit(solution)/shard_map/ppermute | solution.py:639
  137.0 5.1 %collective-permute-start.25 = (f32[8,128]{1,0:T(8,128)S(1)}, f32[8,128]{1,0:T(8,128)S(1)}, u32[]{:S(2)}, u32[]{:S(2)}) collective-permute-start(f32[8,128]{1,0:T(8,128)S(1)} %add_add_fusion.2), channel_id=1, source_target_pairs={{0,2},{1,3},{2,0},{3,1},{4,6},{5,7},{6,4},{7,5},{8,10},{9,11},{10,... | collective-permute-start | bytes 12296 | tf_op jit(solution)/shard_map/ppermute | solution.py:666
  137.0 5.1 %collective-permute-start.24 = (f32[8,128]{1,0:T(8,128)S(1)}, f32[8,128]{1,0:T(8,128)S(1)}, u32[]{:S(2)}, u32[]{:S(2)}) collective-permute-start(f32[8,128]{1,0:T(8,128)S(1)} %add_add_fusion.2), channel_id=1, source_target_pairs={{0,1},{1,2},{2,3},{3,0},{4,5},{5,6},{6,7},{7,4},{8,9},{9,10},{10,1... | collective-permute-start | bytes 12296 | tf_op jit(solution)/shard_map/ppermute | solution.py:666
  145.1 5.1 %collective-permute-start.28 = (f32[8,128]{1,0:T(8,128)S(1)}, f32[8,128]{1,0:T(8,128)S(1)}, u32[]{:S(2)}, u32[]{:S(2)}) collective-permute-start(f32[8,128]{1,0:T(8,128)S(1)} %add_add_fusion.1), channel_id=1, source_target_pairs={{0,8},{1,9},{2,10},{3,11},{4,12},{5,13},{6,14},{7,15},{8,0},{9,1},... | collective-permute-start | bytes 12296 | tf_op jit(solution)/shard_map/ppermute | solution.py:666
  145.1 5.1 %collective-permute-start.27 = (f32[8,128]{1,0:T(8,128)S(1)}, f32[8,128]{1,0:T(8,128)S(1)}, u32[]{:S(2)}, u32[]{:S(2)}) collective-permute-start(f32[8,128]{1,0:T(8,128)S(1)} %add_add_fusion.1), channel_id=1, source_target_pairs={{0,4},{1,5},{2,6},{3,7},{4,8},{5,9},{6,10},{7,11},{8,12},{9,13},{1... | collective-permute-start | bytes 12296 | tf_op jit(solution)/shard_map/ppermute | solution.py:666
  152.5 12.3 %collective-permute-start.16 = (f32[1,32,274]{2,1,0:T(8,128)S(1)}, f32[1,32,274]{2,1,0:T(8,128)S(1)}, u32[]{:S(2)}, u32[]{:S(2)}) collective-permute-start(f32[1,32,274]{2,1,0:T(8,128)S(1)} %get-tuple-element.97), channel_id=1, source_target_pairs={{0,16},{16,32},{32,48},{48,0},{1,17},{17,33},{33,49},{49,1},{2,18}... | collective-permute-start | bytes 105224 | tf_op jit(solution)/shard_map/ppermute | solution.py:639
  153.4 11.4 %collective-permute-start.17 = (f32[1,32,274]{2,1,0:T(8,128)S(1)}, f32[1,32,274]{2,1,0:T(8,128)S(1)}, u32[]{:S(2)}, u32[]{:S(2)}) collective-permute-start(f32[1,32,274]{2,1,0:T(8,128)S(1)} %get-tuple-element.98), channel_id=1, source_target_pairs={{0,48},{16,0},{32,16},{48,32},{1,49},{17,1},{33,17},{49,33},{2,50}... | collective-permute-start | bytes 105224 | tf_op jit(solution)/shard_map/ppermute | solution.py:639
  155.7 9.1 %collective-permute-start.18 = (f32[64,274]{1,0:T(8,128)S(1)}, f32[64,274]{1,0:T(8,128)S(1)}, u32[]{:S(2)}, u32[]{:S(2)}) collective-permute-start(f32[64,274]{1,0:T(8,128)S(1)} %get-tuple-element.99), channel_id=1, source_target_pairs={{0,1},{1,2},{2,3},{3,4},{4,5},{5,6},{6,7},{7,8},{8,9},{9,10},{10,1... | collective-permute-start | bytes 210440 | tf_op jit(solution)/shard_map/ppermute | solution.py:639
  155.9 9.0 %collective-permute-start.19 = (f32[64,274]{1,0:T(8,128)S(1)}, f32[64,274]{1,0:T(8,128)S(1)}, u32[]{:S(2)}, u32[]{:S(2)}) collective-permute-start(f32[64,274]{1,0:T(8,128)S(1)} %get-tuple-element.100), channel_id=1, source_target_pairs={{0,15},{1,0},{2,1},{3,2},{4,3},{5,4},{6,5},{7,6},{8,7},{9,8},{10,9... | collective-permute-start | bytes 210440 | tf_op jit(solution)/shard_map/ppermute | solution.py:639
  (43 other events, 297.6 us)

commit v3 on v2

--- a/solution.py
+++ b/solution.py
@@ -83,13 +83,8 @@
 
 
 def prepare_kernel(
-    side, w_in, w_mid, w_out, cov, in_hi, in_lo, mid_hi, mid_lo, out_hi, out_lo, cov_hi, cov_lo,
-    s_in, s_cov, s_out, s_mid, sems
-):
-    sources = ((w_in, s_in), (cov, s_cov), (w_out, s_out), (w_mid, s_mid))
-    copies = [pltpu.make_async_copy(a, b, sems.at[k]) for k, (a, b) in enumerate(sources)]
-    for copy in copies:
-        copy.start()
+    side, w_in, w_mid, w_out, cov, in_hi, in_lo, mid_hi, mid_lo, out_hi, out_lo, cov_hi, cov_lo
+):
     for target in (in_hi, in_lo, out_hi, out_lo, cov_hi, cov_lo):
         target[...] = jnp.zeros_like(target)
     half = w_in.shape[0] // 2
@@ -105,7 +100,6 @@
         if total % step:
             move(slice(total - total % step, total))
 
-    copies[0].wait()
     for flag in range(2):
 
         @pl.when(side[0] == flag)
@@ -113,32 +107,28 @@
             for target, source in ((0, flag * half), (WIDE, (1 - flag) * half)):
 
                 def move(n, target=target, source=source):
-                    upper, lower = halves_of(s_in[source : source + half, n])
+                    upper, lower = halves_of(w_in[source : source + half, n])
                     in_hi[target : target + half, n] = upper
                     in_lo[target : target + half, n] = lower
 
                 columns(hidden, 128, move)
 
-    copies[1].wait()
-
     def move_cov(n):
-        upper, lower = halves_of(s_cov[:, n])
+        upper, lower = halves_of(cov[:, n])
         cov_hi[:channels, n] = upper
         cov_lo[:channels, n] = lower
 
     columns(channels, 128, move_cov)
-    copies[2].wait()
 
     def move_out(n):
-        upper, lower = halves_of(s_out[:, n])
+        upper, lower = halves_of(w_out[:, n])
         out_hi[:channels, n] = upper
         out_lo[:channels, n] = lower
 
     columns(hidden, 128, move_out)
-    copies[3].wait()
 
     def move_mid(n):
-        upper, lower = halves_of(s_mid[n, :])
+        upper, lower = halves_of(w_mid[n, :])
         mid_hi[n, :] = upper
         mid_lo[n, :] = lower
 
@@ -152,12 +142,11 @@
     return call(
         prepare_kernel,
         out,
-        [smem] + [hbm] * 4,
+        [smem] + [vmem] * 4,
         [vmem] * 8,
-        [pltpu.VMEM(m.shape, f32) for m in (w_in, cov, w_out, w_mid)]
-        + [pltpu.SemaphoreType.DMA((4,))],
-        16,
-        5,
+        [],
+        4,
+        3,
     )(side, w_in, w_mid, w_out, cov)
 
 
@@ -687,21 +676,24 @@
     halo = exchanged(
         right_side[:1], right_side[lats - 1 :], right_side[:, 0], right_side[:, lons - 1]
     )
-    latitude = lax.axis_index("row") * lats + jnp.arange(lats)[None, :, None]
-    plane = jnp.arange(4)[:, None, None]
-    closed = (plane == 2) & (latitude == lats * lax.axis_size("row") - 1)
-    closed = closed | ((plane == 3) & (latitude == 0))
-    planes = jnp.where(closed, 0.0, couplings)
-    planes = jnp.concatenate([planes, jnp.sum(planes, axis=0, keepdims=True)], axis=0)
-    coupling = jnp.transpose(planes, (1, 2, 0))
+    latitude = lax.axis_index("row") * lats + jnp.arange(lats)
+    north_open = (latitude < lats * lax.axis_size("row") - 1)[:, None]
+    south_open = (latitude > 0)[:, None]
+    planes = [
+        couplings[0],
+        couplings[1],
+        jnp.where(north_open, couplings[2], 0.0),
+        jnp.where(south_open, couplings[3], 0.0),
+    ]
+    planes.append(planes[0] + planes[1] + planes[2] + planes[3])
+    coupling = jnp.stack(planes, axis=2)
     pick = ((0, lons - 1), (1, 0), (1, 1), (2, 0), (3, 0), (4, 0))
     pick += ((0, lons - 2), (2, lons - 1), (3, lons - 1), (4, lons - 1))
     columns = jnp.stack([planes[k][:, j] for k, j in pick], axis=1)
     rates = channel_rates[None, :]
     order = jnp.stack([side_index, 1 - side_index])
-    cells = jnp.where(side_index == 0, profile_cells, profile_cells[::-1])
-    cells = jnp.clip(cells, 0, lats * lons - 1)
-    pieces = cells.reshape(2, -1, BLOCK).transpose(1, 0, 2).reshape(-1, BLOCK)
+    cells = jnp.clip(profile_cells[order], 0, lats * lons - 1)
+    pieces = jnp.concatenate([cells[:, k : k + BLOCK] for k in range(0, cells.shape[1], BLOCK)], axis=0)
     counts = profile_counts[order * tile_count + tile_index]
     weights = prepare_call(
         order[:1], weight_in, weight_mid, weight_out.T, inverse_cov, 3 * BLOCK

time: 171 us -> 158 us (0.924)
  local copies, waits for them, and re-layouts: 19.2 us -> 8.88 us
  Pallas kernels: 84 us -> 80.7 us
    unnamed x76 -> x64, local copies, waits for them, and re-layouts: 12.2 us -> 3.49 us
where the time goes in v3:
time: 158 us; the launch traced here: 157 us
  Pallas kernels  80.7 us (51%)
  starting transfers between devices  45.4 us (29%)
  waiting for transfers between devices  18.4 us (12%)
  local copies, waits for them, and re-layouts  8.88 us (6%)
  other arithmetic  2.36 us (1%)
    ppermute x19, starting transfers between devices, shifted(): lax.ppermute(value, axis, [(i, (i + step) % count) for i in range(count)])  37.5 us
    pallas_call x2, Pallas kernels, forward_call(): call(functools.partial(forward_kernel, with_sums), out, [smem] + [vmem] *...  27.8 us
    pallas_call x2, Pallas kernels, backward_call(): call(backward_kernel, [shape((rows, hidden), bf16)] * 2, [vmem] * len(arg...  14.9 us
    pallas_call x2, Pallas kernels, tangent_call(): call(functools.partial(tangent_kernel, with_square), out, [smem, smem] +...  8.99 us
    ppermute x6, waiting for transfers between devices, everyone(): total = total + lax.ppermute(base, 'col', pairs)  8.33 us
    pallas_call x2, Pallas kernels, spread_call(): call(spread_kernel, [shape((lats, lons, width))], [smem] + [vmem] * 2, [v...  7.5 us
    ppermute x6, starting transfers between devices, everyone(): total = total + lax.ppermute(base, 'col', pairs)  6.45 us
    ppermute x5, waiting for transfers between devices, swapped(): return lax.ppermute(value, 'side', [(0, 1), (1, 0)])  5.79 us
  transfers between devices with their start and end apart: 30, of which 10 were waited for; matrix products, arithmetic and copies ran while one was open for 5% of the time, Pallas kernels for 9%

profile of v3, /device:TPU:0, one launch (start us, length us, event | category | flops | bytes accessed | tf_op | source)
XLA Modules:
  0.0 157.3 jit_solution(8045794525339633409)
XLA Ops:
  1.5 2.9 %collective-permute-start.1 = (f32[1,32,274]{2,1,0:T(8,128)S(1)}, f32[1,32,274]{2,1,0:T(8,128)S(1)}, u32[]{:S(2)}, u32[]{:S(2)}) collective-permute-start(f32[1,32,274]{2,1,0:T(8,128)S(1)} %get-tuple-element.107), channel_id=1, source_target_pairs={{0,48},{16,0},{32,16},{48,32},{1,49},{17,1},{33,17},{49,33},{2,50}... | collective-permute-start | bytes 105224 | tf_op jit(solution)/shard_map/ppermute | solution.py:628
  8.0 4.7 %collective-permute-start.3 = (f32[64,274]{1,0:T(8,128)S(1)}, f32[64,274]{1,0:T(8,128)S(1)}, u32[]{:S(2)}, u32[]{:S(2)}) collective-permute-start(f32[64,274]{1,0:T(8,128)S(1)} %bitcast.54), channel_id=1, source_target_pairs={{0,15},{1,0},{2,1},{3,2},{4,3},{5,4},{6,5},{7,6},{8,7},{9,8},{10,9... | collective-permute-start | bytes 210440 | tf_op jit(solution)/shard_map/ppermute | solution.py:628
  21.2 4.6 %shard_map.122 = (f32[512,384]{1,0:T(8,128)S(1)}, f32[512,384]{1,0:T(8,128)S(1)}, f32[8,128]{1,0:T(8,128)S(1)}) custom-call(s32[2,512]{1,0:T(2,128)S(1)} %broadcast_clamp_fusion.cells, s32[2]{0:T(128)S(1)} %gather_fusion, f32[64,32,274]{2,1,0:T(8,128)S(1)} %copy-done.2, f32[1,32,274]{2,1,0:T(8,128)S(1)} %collective-permute-done.south, ...), custom_call_target="tpu_custom_call" | custom-call | flops 6000000000 | bytes 18000000 | tf_op jit(solution)/shard_map/pallas_call | solution.py:211
  26.0 3.2 %shard_map.123 = (bf16[768,1024]{1,0:T(8,128)(2,1)S(1)}, bf16[768,1024]{1,0:T(8,128)(2,1)S(1)}, bf16[1024,1024]{1,0:T(8,128)(2,1)S(1)}, bf16[1024,1024]{1,0:T(8,...) custom-call(s32[1]{0:T(128)} %bitcast.10.side, ...), custom_call_target="tpu_custom_call" | custom-call | flops 3000000000 | bytes 9000000 | tf_op jit(solution)/shard_map/pallas_call | solution.py:142
  29.3 13.7 %shard_map.124 = (bf16[512,768]{1,0:T(8,128)(2,1)S(1)}, bf16[512,768]{1,0:T(8,128)(2,1)S(1)}) custom-call(s32[2]{0:T(128)S(1)} %gather_fusion, f32[512,384]{1,0:T(8,128)S(1)} %get-tuple-element.52.own, f32[512,384]{1,0:T(8,128)S(1)} %collective-permute-done.4.other, bf16[512,1024]{1,0:T(8,128)(2,1)S(1)} %copy-done.8, bf16[512,1024]{1,0:T(8,128)(2,1)S(1)} %copy-done.10, ...), custom_call_target="tpu_custom_call" | custom-call | flops 12999999488 | bytes 39000000 | tf_op jit(solution)/shard_map/pallas_call | solution.py:328
  43.1 7.5 %shard_map.125 = (bf16[512,1024]{1,0:T(8,128)(2,1)S(1)}, bf16[512,1024]{1,0:T(8,128)(2,1)S(1)}) custom-call(bf16[512,768]{1,0:T(8,128)(2,1)S(1)} %get-tuple-element.62.z_hi, bf16[512,768]{1,0:T(8,128)(2,1)S(1)} %get-tuple-element.63.z_lo, bf16[512,1024]{1,0:T(8,128)(2,1)S(1)} %copy-done.8, bf16[512,1024]{1,0:T(8,128)(2,1)S(1)} %copy-done.10, ...), custom_call_target="tpu_custom_call" | custom-call | flops 8000000000 | bytes 24000000 | tf_op jit(solution)/shard_map/pallas_call | solution.py:348
  50.6 2.7 %shard_map.126 = (f32[512,384]{1,0:T(8,128)S(1)}, f32[512,384]{1,0:T(8,128)S(1)}) custom-call(bf16[512,1024]{1,0:T(8,128)(2,1)S(1)} %get-tuple-element.64.b_hi, bf16[512,1024]{1,0:T(8,128)(2,1)S(1)} %get-tuple-element.65.b_lo, bf16[768,1024]{1,0:T(8,128)(2,1)S(1)} %get-tuple-element.54.in_hi, bf16[768,1024]{1,0:T(8,128)(2,1)S(1)} %get-tuple-element.55.in_lo), custom_call_target="tpu_custom_call" | custom-call | flops 3000000000 | bytes 9000000 | tf_op jit(solution)/shard_map/pallas_call | solution.py:361
  57.9 3.0 %collective-permute-start.7 = (f32[1,32,274]{2,1,0:T(8,128)S(1)}, f32[1,32,274]{2,1,0:T(8,128)S(1)}, u32[]{:S(2)}, u32[]{:S(2)}) collective-permute-start(f32[1,32,274]{2,1,0:T(8,128)S(1)} %get-tuple-element.70), channel_id=1, source_target_pairs={{0,48},{16,0},{32,16},{48,32},{1,49},{17,1},{33,17},{49,33},{2,50}... | collective-permute-start | bytes 105224 | tf_op jit(solution)/shard_map/ppermute | solution.py:628
  60.8 5.3 %collective-permute-start.9 = (f32[64,274]{1,0:T(8,128)S(1)}, f32[64,274]{1,0:T(8,128)S(1)}, u32[]{:S(2)}, u32[]{:S(2)}) collective-permute-start(f32[64,274]{1,0:T(8,128)S(1)} %get-tuple-element.72), channel_id=1, source_target_pairs={{0,15},{1,0},{2,1},{3,2},{4,3},{5,4},{6,5},{7,6},{8,7},{9,8},{10,9... | collective-permute-start | bytes 210440 | tf_op jit(solution)/shard_map/ppermute | solution.py:628
  66.2 3.7 %shard_map.128.field = f32[64,32,274]{2,1,0:T(8,128)S(1)} custom-call(s32[2]{0:T(128)S(1)} %gather_fusion, s32[4,256]{1,0:T(4,128)S(1)} %pad_add_fusion.cells, bf16[4,256,768]{2,1,0:T(8,128)(2,1)S(1)} %get-tuple-element.68.parts), custom_call_target="tpu_custom_call" | custom-call | flops 4000000000 | bytes 12000000 | tf_op jit(solution)/shard_map/pallas_call | solution.py:472
  70.3 3.2 %collective-permute-start.11 = (f32[1,32,274]{2,1,0:T(8,128)S(1)}, f32[1,32,274]{2,1,0:T(8,128)S(1)}, u32[]{:S(2)}, u32[]{:S(2)}) collective-permute-start(f32[1,32,274]{2,1,0:T(8,128)S(1)} %get-tuple-element.84), channel_id=1, source_target_pairs={{0,48},{16,0},{32,16},{48,32},{1,49},{17,1},{33,17},{49,33},{2,50}... | collective-permute-start | bytes 105224 | tf_op jit(solution)/shard_map/ppermute | solution.py:628
  73.6 5.3 %collective-permute-start.13 = (f32[64,274]{1,0:T(8,128)S(1)}, f32[64,274]{1,0:T(8,128)S(1)}, u32[]{:S(2)}, u32[]{:S(2)}) collective-permute-start(f32[64,274]{1,0:T(8,128)S(1)} %get-tuple-element.86), channel_id=1, source_target_pairs={{0,15},{1,0},{2,1},{3,2},{4,3},{5,4},{6,5},{7,6},{8,7},{9,8},{10,9... | collective-permute-start | bytes 210440 | tf_op jit(solution)/shard_map/ppermute | solution.py:628
  78.9 3.7 %shard_map.129 = (f32[64,32,274]{2,1,0:T(8,128)S(1)}, f32[8,128]{1,0:T(8,128)S(1)}) custom-call(f32[64,32,274]{2,1,0:T(8,128)S(1)} %shard_map.128.field, f32[1,32,274]{2,1,0:T(8,128)S(1)} %collective-permute-done.6.south, f32[1,32,274]{2,1,0:T(8,128)S(1)} %collective-permute-done.7.north, f32[64,274]{1,0:T(8,128)S(1)} %collective-permute-done.8.west, ...), custom_call_target="tpu_custom_call" | custom-call | flops 5000000000 | bytes 15000000 | tf_op jit(solution)/shard_map/pallas_call | solution.py:565
  82.8 4.4 %shard_map.131 = (f32[512,384]{1,0:T(8,128)S(1)}, f32[512,384]{1,0:T(8,128)S(1)}) custom-call(s32[2,512]{1,0:T(2,128)S(1)} %broadcast_clamp_fusion.cells, s32[2]{0:T(128)S(1)} %gather_fusion, f32[64,32,274]{2,1,0:T(8,128)S(1)} %get-tuple-element.74.field.basis, f32[1,32,274]{2,1,0:T(8,128)S(1)} %collective-permute-done.10.south, ...), custom_call_target="tpu_custom_call" | custom-call | flops 6000000000 | bytes 18000000 | tf_op jit(solution)/shard_map/pallas_call | solution.py:211
  89.6 14.0 %shard_map.132 = (bf16[512,768]{1,0:T(8,128)(2,1)S(1)}, bf16[512,768]{1,0:T(8,128)(2,1)S(1)}, f32[8,128]{1,0:T(8,128)S(1)}) custom-call(s32[2]{0:T(128)S(1)} %gather_fusion, f32[512,384]{1,0:T(8,128)S(1)} %get-tuple-element.87.own, f32[512,384]{1,0:T(8,128)S(1)} %collective-permute-done.14.other, bf16[512,1024]{1,0:T(8,128)(2,1)S(1)} %copy-done.9, ...), custom_call_target="tpu_custom_call" | custom-call | flops 12999999488 | bytes 39000000 | tf_op jit(solution)/shard_map/pallas_call | solution.py:328
  103.6 7.5 %shard_map.133 = (bf16[512,1024]{1,0:T(8,128)(2,1)S(1)}, bf16[512,1024]{1,0:T(8,128)(2,1)S(1)}) custom-call(bf16[512,768]{1,0:T(8,128)(2,1)S(1)} %get-tuple-element.90.z_hi, bf16[512,768]{1,0:T(8,128)(2,1)S(1)} %get-tuple-element.91.z_lo, bf16[512,1024]{1,0:T(8,128)(2,1)S(1)} %copy-done.9, bf16[512,1024]{1,0:T(8,128)(2,1)S(1)} %copy-done.11, ...), custom_call_target="tpu_custom_call" | custom-call | flops 8000000000 | bytes 24000000 | tf_op jit(solution)/shard_map/pallas_call | solution.py:348
  111.1 2.6 %shard_map.134 = (f32[512,384]{1,0:T(8,128)S(1)}, f32[512,384]{1,0:T(8,128)S(1)}) custom-call(bf16[512,1024]{1,0:T(8,128)(2,1)S(1)} %get-tuple-element.92.b_hi, bf16[512,1024]{1,0:T(8,128)(2,1)S(1)} %get-tuple-element.93.b_lo, bf16[768,1024]{1,0:T(8,128)(2,1)S(1)} %copy-done.17, bf16[768,1024]{1,0:T(8,128)(2,1)S(1)} %copy-done.19), custom_call_target="tpu_custom_call" | custom-call | flops 3000000000 | bytes 9000000 | tf_op jit(solution)/shard_map/pallas_call | solution.py:361
  126.0 3.1 %collective-permute-done.25 = f32[8,128]{1,0:T(8,128)S(1)} collective-permute-done((f32[8,128]{1,0:T(8,128)S(1)}, f32[8,128]{1,0:T(8,128)S(1)}, u32[]{:S(2)}, u32[]{:S(2)}) %collective-permute-start.25) | collective-permute-done | bytes 4128 | tf_op jit(solution)/shard_map/ppermute | solution.py:655
  129.1 3.0 %collective-permute-start.29 = (f32[8,128]{1,0:T(8,128)S(1)}, f32[8,128]{1,0:T(8,128)S(1)}, u32[]{:S(2)}, u32[]{:S(2)}) collective-permute-start(f32[8,128]{1,0:T(8,128)S(1)} %add_add_fusion.2), channel_id=1, source_target_pairs={{0,12},{1,13},{2,14},{3,15},{4,0},{5,1},{6,2},{7,3},{8,4},{9,5},{1... | collective-permute-start | bytes 12296 | tf_op jit(solution)/shard_map/ppermute | solution.py:655
  133.4 3.8 %collective-permute-done.28 = f32[8,128]{1,0:T(8,128)S(1)} collective-permute-done((f32[8,128]{1,0:T(8,128)S(1)}, f32[8,128]{1,0:T(8,128)S(1)}, u32[]{:S(2)}, u32[]{:S(2)}) %collective-permute-start.28) | collective-permute-done | bytes 4128 | tf_op jit(solution)/shard_map/ppermute | solution.py:655
  140.4 2.3 %collective-permute-start.17 = (f32[1,32,274]{2,1,0:T(8,128)S(1)}, f32[1,32,274]{2,1,0:T(8,128)S(1)}, u32[]{:S(2)}, u32[]{:S(2)}) collective-permute-start(f32[1,32,274]{2,1,0:T(8,128)S(1)} %get-tuple-element.98), channel_id=1, source_target_pairs={{0,48},{16,0},{32,16},{48,32},{1,49},{17,1},{33,17},{49,33},{2,50}... | collective-permute-start | bytes 105224 | tf_op jit(solution)/shard_map/ppermute | solution.py:628
  142.9 5.2 %collective-permute-start.19 = (f32[64,274]{1,0:T(8,128)S(1)}, f32[64,274]{1,0:T(8,128)S(1)}, u32[]{:S(2)}, u32[]{:S(2)}) collective-permute-start(f32[64,274]{1,0:T(8,128)S(1)} %get-tuple-element.100), channel_id=1, source_target_pairs={{0,15},{1,0},{2,1},{3,2},{4,3},{5,4},{6,5},{7,6},{8,7},{9,8},{10,9... | collective-permute-start | bytes 210440 | tf_op jit(solution)/shard_map/ppermute | solution.py:628
  148.1 3.8 %shard_map.136.field = f32[64,32,274]{2,1,0:T(8,128)S(1)} custom-call(s32[2]{0:T(128)S(1)} %gather_fusion, s32[4,256]{1,0:T(4,128)S(1)} %pad_add_fusion.cells, bf16[4,256,768]{2,1,0:T(8,128)(2,1)S(1)} %get-tuple-element.96.parts), custom_call_target="tpu_custom_call" | custom-call | flops 4000000000 | bytes 12000000 | tf_op jit(solution)/shard_map/pallas_call | solution.py:472
  151.9 5.3 %shard_map.137 = (f32[64,32,274]{2,1,0:T(8,128)}, f32[64,32,274]{2,1,0:T(8,128)}) custom-call(f32[64,32,274]{2,1,0:T(8,128)S(1)} %shard_map.136.field, f32[1,32,274]{2,1,0:T(8,128)S(1)} %collective-permute-done.16.south, f32[1,32,274]{2,1,0:T(8,128)S(1)} %collective-permute-done.17.north, f32[64,274]{1,0:T(8,128)S(1)} %collective-permute-done.18.west, ...), custom_call_target="tpu_custom_call" | custom-call | flops 6000000000 | bytes 18000000 | tf_op jit(solution)/shard_map/pallas_call | solution.py:615
  (145 shorter events, 37.4 us)
Async XLA Ops:
  1.5 17.8 %collective-permute-start.1 = (f32[1,32,274]{2,1,0:T(8,128)S(1)}, f32[1,32,274]{2,1,0:T(8,128)S(1)}, u32[]{:S(2)}, u32[]{:S(2)}) collective-permute-start(f32[1,32,274]{2,1,0:T(8,128)S(1)} %get-tuple-element.107), channel_id=1, source_target_pairs={{0,48},{16,0},{32,16},{48,32},{1,49},{17,1},{33,17},{49,33},{2,50}... | collective-permute-start | bytes 105224 | tf_op jit(solution)/shard_map/ppermute | solution.py:628
  4.4 14.9 %collective-permute-start = (f32[1,32,274]{2,1,0:T(8,128)S(1)}, f32[1,32,274]{2,1,0:T(8,128)S(1)}, u32[]{:S(2)}, u32[]{:S(2)}) collective-permute-start(f32[1,32,274]{2,1,0:T(8,128)S(1)} %get-tuple-element.108), channel_id=1, source_target_pairs={{0,16},{16,32},{32,48},{48,0},{1,17},{17,33},{33,49},{49,1},{2,18}... | collective-permute-start | bytes 105224 | tf_op jit(solution)/shard_map/ppermute | solution.py:628
  6.0 13.3 %collective-permute-start.2 = (f32[64,274]{1,0:T(8,128)S(1)}, f32[64,274]{1,0:T(8,128)S(1)}, u32[]{:S(2)}, u32[]{:S(2)}) collective-permute-start(f32[64,274]{1,0:T(8,128)S(1)} %bitcast.53), channel_id=1, source_target_pairs={{0,1},{1,2},{2,3},{3,4},{4,5},{5,6},{6,7},{7,8},{8,9},{9,10},{10,1... | collective-permute-start | bytes 210440 | tf_op jit(solution)/shard_map/ppermute | solution.py:628
  8.0 11.4 %collective-permute-start.3 = (f32[64,274]{1,0:T(8,128)S(1)}, f32[64,274]{1,0:T(8,128)S(1)}, u32[]{:S(2)}, u32[]{:S(2)}) collective-permute-start(f32[64,274]{1,0:T(8,128)S(1)} %bitcast.54), channel_id=1, source_target_pairs={{0,15},{1,0},{2,1},{3,2},{4,3},{5,4},{6,5},{7,6},{8,7},{9,8},{10,9... | collective-permute-start | bytes 210440 | tf_op jit(solution)/shard_map/ppermute | solution.py:628
  57.5 12.4 %collective-permute-start.6 = (f32[1,32,274]{2,1,0:T(8,128)S(1)}, f32[1,32,274]{2,1,0:T(8,128)S(1)}, u32[]{:S(2)}, u32[]{:S(2)}) collective-permute-start(f32[1,32,274]{2,1,0:T(8,128)S(1)} %get-tuple-element.69), channel_id=1, source_target_pairs={{0,16},{16,32},{32,48},{48,0},{1,17},{17,33},{33,49},{49,1},{2,18}... | collective-permute-start | bytes 105224 | tf_op jit(solution)/shard_map/ppermute | solution.py:628
  57.9 12.1 %collective-permute-start.7 = (f32[1,32,274]{2,1,0:T(8,128)S(1)}, f32[1,32,274]{2,1,0:T(8,128)S(1)}, u32[]{:S(2)}, u32[]{:S(2)}) collective-permute-start(f32[1,32,274]{2,1,0:T(8,128)S(1)} %get-tuple-element.70), channel_id=1, source_target_pairs={{0,48},{16,0},{32,16},{48,32},{1,49},{17,1},{33,17},{49,33},{2,50}... | collective-permute-start | bytes 105224 | tf_op jit(solution)/shard_map/ppermute | solution.py:628
  60.8 9.1 %collective-permute-start.8 = (f32[64,274]{1,0:T(8,128)S(1)}, f32[64,274]{1,0:T(8,128)S(1)}, u32[]{:S(2)}, u32[]{:S(2)}) collective-permute-start(f32[64,274]{1,0:T(8,128)S(1)} %get-tuple-element.71), channel_id=1, source_target_pairs={{0,1},{1,2},{2,3},{3,4},{4,5},{5,6},{6,7},{7,8},{8,9},{9,10},{10,1... | collective-permute-start | bytes 210440 | tf_op jit(solution)/shard_map/ppermute | solution.py:628
  60.8 9.1 %collective-permute-start.9 = (f32[64,274]{1,0:T(8,128)S(1)}, f32[64,274]{1,0:T(8,128)S(1)}, u32[]{:S(2)}, u32[]{:S(2)}) collective-permute-start(f32[64,274]{1,0:T(8,128)S(1)} %get-tuple-element.72), channel_id=1, source_target_pairs={{0,15},{1,0},{2,1},{3,2},{4,3},{5,4},{6,5},{7,6},{8,7},{9,8},{10,9... | collective-permute-start | bytes 210440 | tf_op jit(solution)/shard_map/ppermute | solution.py:628
  70.2 12.4 %collective-permute-start.10 = (f32[1,32,274]{2,1,0:T(8,128)S(1)}, f32[1,32,274]{2,1,0:T(8,128)S(1)}, u32[]{:S(2)}, u32[]{:S(2)}) collective-permute-start(f32[1,32,274]{2,1,0:T(8,128)S(1)} %get-tuple-element.83), channel_id=1, source_target_pairs={{0,16},{16,32},{32,48},{48,0},{1,17},{17,33},{33,49},{49,1},{2,18}... | collective-permute-start | bytes 105224 | tf_op jit(solution)/shard_map/ppermute | solution.py:628
  70.3 12.3 %collective-permute-start.11 = (f32[1,32,274]{2,1,0:T(8,128)S(1)}, f32[1,32,274]{2,1,0:T(8,128)S(1)}, u32[]{:S(2)}, u32[]{:S(2)}) collective-permute-start(f32[1,32,274]{2,1,0:T(8,128)S(1)} %get-tuple-element.84), channel_id=1, source_target_pairs={{0,48},{16,0},{32,16},{48,32},{1,49},{17,1},{33,17},{49,33},{2,50}... | collective-permute-start | bytes 105224 | tf_op jit(solution)/shard_map/ppermute | solution.py:628
  73.6 9.1 %collective-permute-start.12 = (f32[64,274]{1,0:T(8,128)S(1)}, f32[64,274]{1,0:T(8,128)S(1)}, u32[]{:S(2)}, u32[]{:S(2)}) collective-permute-start(f32[64,274]{1,0:T(8,128)S(1)} %get-tuple-element.85), channel_id=1, source_target_pairs={{0,1},{1,2},{2,3},{3,4},{4,5},{5,6},{6,7},{7,8},{8,9},{9,10},{10,1... | collective-permute-start | bytes 210440 | tf_op jit(solution)/shard_map/ppermute | solution.py:628
  73.6 9.1 %collective-permute-start.13 = (f32[64,274]{1,0:T(8,128)S(1)}, f32[64,274]{1,0:T(8,128)S(1)}, u32[]{:S(2)}, u32[]{:S(2)}) collective-permute-start(f32[64,274]{1,0:T(8,128)S(1)} %get-tuple-element.86), channel_id=1, source_target_pairs={{0,15},{1,0},{2,1},{3,2},{4,3},{5,4},{6,5},{7,6},{8,7},{9,8},{10,9... | collective-permute-start | bytes 210440 | tf_op jit(solution)/shard_map/ppermute | solution.py:628
  113.7 23.5 %collective-permute-start.15 = (f32[512,384]{1,0:T(8,128)S(1)}, f32[512,384]{1,0:T(8,128)S(1)}, u32[]{:S(2)}, u32[]{:S(2)}) collective-permute-start(f32[512,384]{1,0:T(8,128)S(1)} %get-tuple-element.95), channel_id=1, source_target_pairs={{0,64},{64,0},{1,65},{65,1},{2,66},{66,2},{3,67},{67,3},{4,68},{68... | collective-permute-start | bytes 2359304 | tf_op jit(solution)/shard_map/ppermute | solution.py:640
  116.1 5.1 %collective-permute-start.22 = (f32[8,128]{1,0:T(8,128)S(1)}, f32[8,128]{1,0:T(8,128)S(1)}, u32[]{:S(2)}, u32[]{:S(2)}) collective-permute-start(f32[8,128]{1,0:T(8,128)S(1)} %add.128), channel_id=1, source_target_pairs={{0,32},{16,48},{32,0},{48,16},{1,33},{17,49},{33,1},{49,17},{2,34}... | collective-permute-start | bytes 12296 | tf_op jit(solution)/shard_map/ppermute | solution.py:628
  116.6 5.8 %collective-permute-start.21 = (f32[8,128]{1,0:T(8,128)S(1)}, f32[8,128]{1,0:T(8,128)S(1)}, u32[]{:S(2)}, u32[]{:S(2)}) collective-permute-start(f32[8,128]{1,0:T(8,128)S(1)} %add.128), channel_id=1, source_target_pairs={{0,16},{16,32},{32,48},{48,0},{1,17},{17,33},{33,49},{49,1},{2,18}... | collective-permute-start | bytes 12296 | tf_op jit(solution)/shard_map/ppermute | solution.py:628
  124.0 5.1 %collective-permute-start.25 = (f32[8,128]{1,0:T(8,128)S(1)}, f32[8,128]{1,0:T(8,128)S(1)}, u32[]{:S(2)}, u32[]{:S(2)}) collective-permute-start(f32[8,128]{1,0:T(8,128)S(1)} %add_add_fusion.3), channel_id=1, source_target_pairs={{0,2},{1,3},{2,0},{3,1},{4,6},{5,7},{6,4},{7,5},{8,10},{9,11},{10,... | collective-permute-start | bytes 12296 | tf_op jit(solution)/shard_map/ppermute | solution.py:655
  124.0 5.1 %collective-permute-start.24 = (f32[8,128]{1,0:T(8,128)S(1)}, f32[8,128]{1,0:T(8,128)S(1)}, u32[]{:S(2)}, u32[]{:S(2)}) collective-permute-start(f32[8,128]{1,0:T(8,128)S(1)} %add_add_fusion.3), channel_id=1, source_target_pairs={{0,1},{1,2},{2,3},{3,0},{4,5},{5,6},{6,7},{7,4},{8,9},{9,10},{10,1... | collective-permute-start | bytes 12296 | tf_op jit(solution)/shard_map/ppermute | solution.py:655
  129.1 4.3 %collective-permute-start.29 = (f32[8,128]{1,0:T(8,128)S(1)}, f32[8,128]{1,0:T(8,128)S(1)}, u32[]{:S(2)}, u32[]{:S(2)}) collective-permute-start(f32[8,128]{1,0:T(8,128)S(1)} %add_add_fusion.2), channel_id=1, source_target_pairs={{0,12},{1,13},{2,14},{3,15},{4,0},{5,1},{6,2},{7,3},{8,4},{9,5},{1... | collective-permute-start | bytes 12296 | tf_op jit(solution)/shard_map/ppermute | solution.py:655
  132.1 5.1 %collective-permute-start.28 = (f32[8,128]{1,0:T(8,128)S(1)}, f32[8,128]{1,0:T(8,128)S(1)}, u32[]{:S(2)}, u32[]{:S(2)}) collective-permute-start(f32[8,128]{1,0:T(8,128)S(1)} %add_add_fusion.2), channel_id=1, source_target_pairs={{0,8},{1,9},{2,10},{3,11},{4,12},{5,13},{6,14},{7,15},{8,0},{9,1},... | collective-permute-start | bytes 12296 | tf_op jit(solution)/shard_map/ppermute | solution.py:655
  132.1 5.1 %collective-permute-start.27 = (f32[8,128]{1,0:T(8,128)S(1)}, f32[8,128]{1,0:T(8,128)S(1)}, u32[]{:S(2)}, u32[]{:S(2)}) collective-permute-start(f32[8,128]{1,0:T(8,128)S(1)} %add_add_fusion.2), channel_id=1, source_target_pairs={{0,4},{1,5},{2,6},{3,7},{4,8},{5,9},{6,10},{7,11},{8,12},{9,13},{1... | collective-permute-start | bytes 12296 | tf_op jit(solution)/shard_map/ppermute | solution.py:655
  139.5 12.3 %collective-permute-start.16 = (f32[1,32,274]{2,1,0:T(8,128)S(1)}, f32[1,32,274]{2,1,0:T(8,128)S(1)}, u32[]{:S(2)}, u32[]{:S(2)}) collective-permute-start(f32[1,32,274]{2,1,0:T(8,128)S(1)} %get-tuple-element.97), channel_id=1, source_target_pairs={{0,16},{16,32},{32,48},{48,0},{1,17},{17,33},{33,49},{49,1},{2,18}... | collective-permute-start | bytes 105224 | tf_op jit(solution)/shard_map/ppermute | solution.py:628
  140.4 11.4 %collective-permute-start.17 = (f32[1,32,274]{2,1,0:T(8,128)S(1)}, f32[1,32,274]{2,1,0:T(8,128)S(1)}, u32[]{:S(2)}, u32[]{:S(2)}) collective-permute-start(f32[1,32,274]{2,1,0:T(8,128)S(1)} %get-tuple-element.98), channel_id=1, source_target_pairs={{0,48},{16,0},{32,16},{48,32},{1,49},{17,1},{33,17},{49,33},{2,50}... | collective-permute-start | bytes 105224 | tf_op jit(solution)/shard_map/ppermute | solution.py:628
  142.7 9.1 %collective-permute-start.18 = (f32[64,274]{1,0:T(8,128)S(1)}, f32[64,274]{1,0:T(8,128)S(1)}, u32[]{:S(2)}, u32[]{:S(2)}) collective-permute-start(f32[64,274]{1,0:T(8,128)S(1)} %get-tuple-element.99), channel_id=1, source_target_pairs={{0,1},{1,2},{2,3},{3,4},{4,5},{5,6},{6,7},{7,8},{8,9},{9,10},{10,1... | collective-permute-start | bytes 210440 | tf_op jit(solution)/shard_map/ppermute | solution.py:628
  142.9 9.0 %collective-permute-start.19 = (f32[64,274]{1,0:T(8,128)S(1)}, f32[64,274]{1,0:T(8,128)S(1)}, u32[]{:S(2)}, u32[]{:S(2)}) collective-permute-start(f32[64,274]{1,0:T(8,128)S(1)} %get-tuple-element.100), channel_id=1, source_target_pairs={{0,15},{1,0},{2,1},{3,2},{4,3},{5,4},{6,5},{7,6},{8,7},{9,8},{10,9... | collective-permute-start | bytes 210440 | tf_op jit(solution)/shard_map/ppermute | solution.py:628
  (36 other events, 295.0 us)
